TPU v7x, 32 devices: a whole 2x2x4 slice. The times are simulated.
32 devices in a mesh: rep: 8 (over z, y), shard: 4 (over x, core).
Axes of the slice: x: 2, y: 2, z: 4, core: 2. Of those that a mesh axis runs over, the one named last changes fastest.
Arguments:
- layer_input: bfloat16 [32, 1024, 1152], P(('rep', 'shard')), may hold values from -6 to 6
- segments: int32 [32, 1024], P(('rep', 'shard')), may hold values from 0 to 15, never falling along the last dimension, each value on 1 to 512 neighbouring positions
- query_weight: bfloat16 [1152, 1152], P('shard'), may hold values from -0.25 to 0.25
- key_weight: bfloat16 [1152, 384], P('shard'), may hold values from -0.25 to 0.25
- value_weight: bfloat16 [1152, 384], P('shard'), may hold values from -0.1875 to 0.1875
- output_weight: bfloat16 [1152, 1152], P('shard'), may hold values from -0.75 to 0.75
- gate_weight: bfloat16 [1152, 3072], P('shard'), may hold values from -0.1875 to 0.1875
- up_weight: bfloat16 [1152, 3072], P('shard'), may hold values from -0.1875 to 0.1875
- down_weight: bfloat16 [3072, 1152], P('shard'), may hold values from -0.109375 to 0.109375
- attention_gain: bfloat16 [1152], P('shard'), may hold values from 0.5 to 1.5
- feedforward_gain: bfloat16 [1152], P('shard'), may hold values from 0.5 to 1.5
- upstream: bfloat16 [32, 1024, 1152], P(('rep', 'shard')), may hold values from -6 to 6
Outputs:
- layer_output: bfloat16 [32, 1024, 1152], P(('rep', 'shard'))
- input_grad: float32 [32, 1024, 1152], P(('rep', 'shard'))
- query_grad: float32 [1152, 1152], P('shard')
- key_grad: float32 [1152, 384], P('shard')
- value_grad: float32 [1152, 384], P('shard')
- output_grad: float32 [1152, 1152], P('shard')
- gate_grad: float32 [1152, 3072], P('shard')
- up_grad: float32 [1152, 3072], P('shard')
- down_grad: float32 [3072, 1152], P('shard')
- attention_gain_grad: float32 [1152], P('shard')
- feedforward_gain_grad: float32 [1152], P('shard')
- head_maxima: float32 [18], replicated
- query_clipped: float32 [1152, 1152], P('shard')
- key_clipped: float32 [1152, 384], P('shard')
Inputs may be any that keep to these rules, and one draw needn't show every extreme that they name: `segments`: segment numbers never fall along a sequence; each document has 1 to 512 tokens.
All inputs are finite; a program needn't handle non-finite values.
Results may differ from a plain program's by a relative error of at most 0.017.
Values may be sent and summed in bfloat16 or wider, within the bound.
A program may use at most 384 MiB of HBM per device.

v0:
```python
import math

import jax
import jax.numpy as jnp
from jax import lax
from jax.sharding import PartitionSpec as P

HEADS = 18
KV_HEADS = 6
HEAD_DIM = 64


eps_norm = 1e-05
rope_base = 10000.0
clip_tau = 2.5
mask_fill = -1000000000.0
floor_fill = -1e30


def positions_of(segment_row):
    position_index = jnp.arange(segment_row.shape[0], dtype=jnp.int32)
    changed = jnp.concatenate(
        [jnp.ones((1,), dtype=jnp.bool_), segment_row[1:] != segment_row[:-1]]
    )
    starts = lax.cummax(jnp.where(changed, position_index, 0), axis=0)
    return position_index - starts


def rope_tables(places):
    half_size = HEAD_DIM // 2
    frequency = rope_base ** (-jnp.arange(half_size, dtype=jnp.float32) * 2.0 / HEAD_DIM)
    angles = places.astype(jnp.float32)[:, None] * frequency[None, :]
    return (jnp.cos(angles)[:, None, :], jnp.sin(angles)[:, None, :])


def rotate(values_in, cosine, sine, head_count):
    row_count = values_in.shape[0]
    half_size = HEAD_DIM // 2
    shaped = values_in.reshape(row_count, head_count, HEAD_DIM)
    first_half = shaped[..., :half_size]
    second_half = shaped[..., half_size:]
    turned = jnp.concatenate(
        [first_half * cosine - second_half * sine, second_half * cosine + first_half * sine],
        axis=-1,
    )
    return turned.reshape(row_count, head_count * HEAD_DIM)


def product(left, right):
    return jnp.dot(left, right, preferred_element_type=jnp.float32)


def product_left(left, right):
    return lax.dot_general(
        left, right, (((0,), (0,)), ((), ())), preferred_element_type=jnp.float32
    )


def product_right(left, right):
    return lax.dot_general(
        left, right, (((1,), (1,)), ((), ())), preferred_element_type=jnp.float32
    )


def attend_forward(query_block, key_heads, value_heads, allowed, score_scale):
    scores = (
        jnp.einsum("qgrd,kgd->grqk", query_block, key_heads, preferred_element_type=jnp.float32)
        * score_scale
    )
    block_top = jnp.max(jnp.where(allowed, scores, floor_fill), axis=(2, 3))
    masked = jnp.where(allowed, scores, mask_fill)
    row_peaks = jnp.max(masked, axis=-1, keepdims=True)
    exponents = jnp.exp(masked - row_peaks)
    totals = jnp.sum(exponents, axis=-1, keepdims=True)
    softmax_weights = (exponents / totals).astype(jnp.bfloat16)
    mixed_heads = jnp.einsum(
        "grqk,kgd->qgrd", softmax_weights, value_heads, preferred_element_type=jnp.float32
    )
    return (mixed_heads, row_peaks + jnp.log(totals), block_top)


def attend_backward(
    query_block, key_heads, value_heads, allowed, log_totals, grad_block, score_scale
):
    scores = (
        jnp.einsum("qgrd,kgd->grqk", query_block, key_heads, preferred_element_type=jnp.float32)
        * score_scale
    )
    softmax_weights = jnp.where(allowed, jnp.exp(scores - log_totals), 0.0)
    grad_weights = jnp.einsum(
        "qgrd,kgd->grqk", grad_block, value_heads, preferred_element_type=jnp.float32
    )
    row_inner = jnp.sum(softmax_weights * grad_weights, axis=-1, keepdims=True)
    grad_scores = (softmax_weights * (grad_weights - row_inner) * score_scale).astype(jnp.bfloat16)
    grad_query = jnp.einsum(
        "grqk,kgd->qgrd", grad_scores, key_heads, preferred_element_type=jnp.float32
    )
    grad_key = jnp.einsum(
        "grqk,qgrd->kgd", grad_scores, query_block, preferred_element_type=jnp.float32
    )
    grad_value = jnp.einsum(
        "grqk,qgrd->kgd",
        softmax_weights.astype(jnp.bfloat16),
        grad_block,
        preferred_element_type=jnp.float32,
    )
    return (grad_query, grad_key, grad_value)


def on_device(
    layer_input,
    segments,
    query_weight,
    key_weight,
    value_weight,
    output_weight,
    gate_weight,
    up_weight,
    down_weight,
    attention_gain,
    feedforward_gain,
    upstream,
):
    seq_count, length, model_width = layer_input.shape
    token_rows = seq_count * length
    group_size = HEADS // KV_HEADS
    query_width = HEADS * HEAD_DIM
    key_width = KV_HEADS * HEAD_DIM
    score_scale = 1.0 / math.sqrt(HEAD_DIM)
    block_rows = 512
    position_index = jnp.arange(length, dtype=jnp.int32)
    query_full, key_full, value_full, output_full, gain_first = (
        lax.all_gather(query_weight, "shard", axis=0, tiled=True),
        lax.all_gather(key_weight, "shard", axis=0, tiled=True),
        lax.all_gather(value_weight, "shard", axis=0, tiled=True),
        lax.all_gather(output_weight, "shard", axis=0, tiled=True),
        lax.all_gather(attention_gain, "shard", axis=0, tiled=True),
    )
    inputs = layer_input.reshape(token_rows, model_width).astype(jnp.float32)
    places = jax.vmap(positions_of)(segments).reshape(token_rows)
    cosine, sine = rope_tables(places)
    first_rstd = lax.rsqrt(jnp.mean(inputs * inputs, axis=-1, keepdims=True) + eps_norm)
    first_unit = inputs * first_rstd
    gain_first_wide = gain_first.astype(jnp.float32)
    first_normed = (first_unit * gain_first_wide).astype(jnp.bfloat16)
    queries = rotate(product(first_normed, query_full), cosine, sine, HEADS).astype(jnp.bfloat16)
    keys_rot = rotate(product(first_normed, key_full), cosine, sine, KV_HEADS).astype(jnp.bfloat16)
    values = product(first_normed, value_full).astype(jnp.bfloat16)
    query_heads = queries.reshape(seq_count, length, KV_HEADS, group_size, HEAD_DIM)
    key_heads = keys_rot.reshape(seq_count, length, KV_HEADS, HEAD_DIM)
    value_heads = values.reshape(seq_count, length, KV_HEADS, HEAD_DIM)
    mixed_parts = []
    log_parts = []
    head_top = jnp.full((KV_HEADS, group_size), floor_fill, jnp.float32)
    sequence = 0
    same_doc = segments[sequence][:, None] == segments[sequence][None, :]
    for row_start in range(0, length, block_rows):
        allowed = same_doc[row_start : row_start + block_rows] & (
            position_index[None, :] <= position_index[row_start : row_start + block_rows, None]
        )
        mixed_block, log_block, block_top = attend_forward(
            query_heads[sequence, row_start : row_start + block_rows],
            key_heads[sequence],
            value_heads[sequence],
            allowed,
            score_scale,
        )
        mixed_parts.append(mixed_block)
        log_parts.append(log_block)
        head_top = jnp.maximum(head_top, block_top)
    maxima = lax.pmax(head_top.reshape(HEADS), ("rep", "shard"))
    mixed = (
        jnp.concatenate(mixed_parts, axis=0).reshape(token_rows, query_width).astype(jnp.bfloat16)
    )
    residual = inputs + product(mixed, output_full)
    gate_full, up_full, down_full, gain_second = (
        lax.all_gather(gate_weight, "shard", axis=0, tiled=True),
        lax.all_gather(up_weight, "shard", axis=0, tiled=True),
        lax.all_gather(down_weight, "shard", axis=0, tiled=True),
        lax.all_gather(feedforward_gain, "shard", axis=0, tiled=True),
    )
    second_rstd = lax.rsqrt(jnp.mean(residual * residual, axis=-1, keepdims=True) + eps_norm)
    second_unit = residual * second_rstd
    gain_second_wide = gain_second.astype(jnp.float32)
    second_normed = (second_unit * gain_second_wide).astype(jnp.bfloat16)
    gate_values = product(second_normed, gate_full)
    up_values = product(second_normed, up_full)
    sigmoid_gate = jax.nn.sigmoid(gate_values)
    swish_gate = gate_values * sigmoid_gate
    activated = (swish_gate * up_values).astype(jnp.bfloat16)
    layer_output = (
        (residual + product(activated, down_full)).astype(jnp.bfloat16).reshape(layer_input.shape)
    )
    gate_back, up_back, down_back = (
        lax.all_gather(gate_weight, "shard", axis=0, tiled=True),
        lax.all_gather(up_weight, "shard", axis=0, tiled=True),
        lax.all_gather(down_weight, "shard", axis=0, tiled=True),
    )
    grad_output = upstream.reshape(token_rows, model_width).astype(jnp.float32)
    grad_down_in = grad_output.astype(jnp.bfloat16)
    grad_activated = product_right(grad_down_in, down_back)
    grad_gate_low = (
        grad_activated * up_values * sigmoid_gate * (1.0 + gate_values * (1.0 - sigmoid_gate))
    ).astype(jnp.bfloat16)
    grad_up_low = (grad_activated * swish_gate).astype(jnp.bfloat16)
    down_term = product_left(activated, grad_down_in)
    gate_term = product_left(second_normed, grad_gate_low)
    up_term = product_left(second_normed, grad_up_low)
    grad_second = product_right(grad_gate_low, gate_back) + product_right(grad_up_low, up_back)
    second_gain_term = jnp.sum(grad_second * second_unit, axis=0)
    grad_unit_second = grad_second * gain_second_wide
    grad_residual = (
        second_rstd
        * (
            grad_unit_second
            - second_unit * jnp.mean(grad_unit_second * second_unit, axis=-1, keepdims=True)
        )
        + grad_output
    )
    feedforward_sums = (
        lax.psum_scatter(
            gate_term.astype(jnp.bfloat16), "shard", scatter_dimension=0, tiled=True
        ).astype(jnp.float32),
        lax.psum_scatter(
            up_term.astype(jnp.bfloat16), "shard", scatter_dimension=0, tiled=True
        ).astype(jnp.float32),
        lax.psum_scatter(
            down_term.astype(jnp.bfloat16), "shard", scatter_dimension=0, tiled=True
        ).astype(jnp.float32),
        lax.psum_scatter(
            second_gain_term.astype(jnp.bfloat16), "shard", scatter_dimension=0, tiled=True
        ).astype(jnp.float32),
    )
    gate_grad, up_grad, down_grad, feedforward_gain_grad = lax.psum(
        (feedforward_sums[0], feedforward_sums[1], feedforward_sums[2], feedforward_sums[3]), "rep"
    )
    query_back, key_back, value_back, output_back = (
        lax.all_gather(query_weight, "shard", axis=0, tiled=True),
        lax.all_gather(key_weight, "shard", axis=0, tiled=True),
        lax.all_gather(value_weight, "shard", axis=0, tiled=True),
        lax.all_gather(output_weight, "shard", axis=0, tiled=True),
    )
    grad_out_in = grad_residual.astype(jnp.bfloat16)
    output_term = product_left(mixed, grad_out_in)
    grad_mixed = product_right(grad_out_in, output_back).astype(jnp.bfloat16)
    grad_heads = grad_mixed.reshape(seq_count, length, KV_HEADS, group_size, HEAD_DIM)
    query_parts = []
    part_number = 0
    sequence = 0
    same_doc = segments[sequence][:, None] == segments[sequence][None, :]
    key_total = jnp.zeros((length, KV_HEADS, HEAD_DIM), jnp.float32)
    value_total = jnp.zeros((length, KV_HEADS, HEAD_DIM), jnp.float32)
    for row_start in range(0, length, block_rows):
        allowed = same_doc[row_start : row_start + block_rows] & (
            position_index[None, :] <= position_index[row_start : row_start + block_rows, None]
        )
        grad_query, grad_key, grad_value = attend_backward(
            query_heads[sequence, row_start : row_start + block_rows],
            key_heads[sequence],
            value_heads[sequence],
            allowed,
            log_parts[part_number],
            grad_heads[sequence, row_start : row_start + block_rows],
            score_scale,
        )
        part_number += 1
        query_parts.append(grad_query)
        key_total = key_total + grad_key
        value_total = value_total + grad_value
    grad_queries = jnp.concatenate(query_parts, axis=0).reshape(token_rows, query_width)
    grad_keys = key_total.reshape(token_rows, key_width)
    grad_values = value_total.reshape(token_rows, key_width)
    query_low = rotate(grad_queries, cosine, -sine, HEADS).astype(jnp.bfloat16)
    key_low = rotate(grad_keys, cosine, -sine, KV_HEADS).astype(jnp.bfloat16)
    value_low = grad_values.astype(jnp.bfloat16)
    query_term = product_left(first_normed, query_low)
    key_term = product_left(first_normed, key_low)
    value_term = product_left(first_normed, value_low)
    grad_first = (
        product_right(query_low, query_back)
        + product_right(key_low, key_back)
        + product_right(value_low, value_back)
    )
    first_gain_term = jnp.sum(grad_first * first_unit, axis=0)
    grad_unit_first = grad_first * gain_first_wide
    input_grad = (
        first_rstd
        * (
            grad_unit_first
            - first_unit * jnp.mean(grad_unit_first * first_unit, axis=-1, keepdims=True)
        )
        + grad_residual
    )
    attention_sums = (
        lax.psum_scatter(
            query_term.astype(jnp.bfloat16), "shard", scatter_dimension=0, tiled=True
        ).astype(jnp.float32),
        lax.psum_scatter(
            key_term.astype(jnp.bfloat16), "shard", scatter_dimension=0, tiled=True
        ).astype(jnp.float32),
        lax.psum_scatter(
            value_term.astype(jnp.bfloat16), "shard", scatter_dimension=0, tiled=True
        ).astype(jnp.float32),
        lax.psum_scatter(
            output_term.astype(jnp.bfloat16), "shard", scatter_dimension=0, tiled=True
        ).astype(jnp.float32),
        lax.psum_scatter(
            first_gain_term.astype(jnp.bfloat16), "shard", scatter_dimension=0, tiled=True
        ).astype(jnp.float32),
    )
    query_grad, key_grad, value_grad, output_grad, attention_gain_grad = lax.psum(
        (
            attention_sums[0],
            attention_sums[1],
            attention_sums[2],
            attention_sums[3],
            attention_sums[4],
        ),
        "rep",
    )
    query_factor = jnp.sqrt(clip_tau / jnp.maximum(maxima, clip_tau))
    key_factor = jnp.sqrt(
        clip_tau / jnp.maximum(jnp.max(maxima.reshape(KV_HEADS, group_size), axis=1), clip_tau)
    )
    local_rows = query_weight.shape[0]
    query_clipped = (
        query_weight.astype(jnp.float32).reshape(local_rows, HEADS, HEAD_DIM)
        * query_factor[None, :, None]
    ).reshape(local_rows, query_width)
    key_clipped = (
        key_weight.astype(jnp.float32).reshape(local_rows, KV_HEADS, HEAD_DIM)
        * key_factor[None, :, None]
    ).reshape(local_rows, key_width)
    return (
        layer_output,
        input_grad.reshape(layer_input.shape),
        query_grad,
        key_grad,
        value_grad,
        output_grad,
        gate_grad,
        up_grad,
        down_grad,
        attention_gain_grad,
        feedforward_gain_grad,
        maxima,
        query_clipped,
        key_clipped,
    )


def solution(mesh):
    return jax.shard_map(
        on_device,
        mesh=mesh,
        in_specs=(
            P(("rep", "shard"), None, None),
            P(("rep", "shard"), None),
            P("shard", None),
            P("shard", None),
            P("shard", None),
            P("shard", None),
            P("shard", None),
            P("shard", None),
            P("shard", None),
            P("shard"),
            P("shard"),
            P(("rep", "shard"), None, None),
        ),
        out_specs=(
            P(("rep", "shard"), None, None),
            P(("rep", "shard"), None, None),
            P("shard", None),
            P("shard", None),
            P("shard", None),
            P("shard", None),
            P("shard", None),
            P("shard", None),
            P("shard", None),
            P("shard"),
            P("shard"),
            P(),
            P("shard", None),
            P("shard", None),
        ),
        check_vma=False,
    )
```

profile of v0, /device:TPU:0, one launch (start us, length us, event | category | flops | bytes accessed | tf_op | source)
XLA Modules:
  0.0 1374.5 jit_solution(2080988262117837409)
XLA Ops:
  14.5 8.5 all-reduce.6
  24.2 14.4 %all_gather.35 = bf16[1152,384]{1,0:T(8,128)(2,1)} all-gather(bf16[288,384]{1,0:T(8,128)(2,1)S(1)} %copy-done.35), channel_id=1, replica_groups=mesh['rep'=8,'shard'=4] {'shard'}, dimensions={0}, use_global_device_ids=true | all-gather | bytes 1105920 | tf_op jit(solution)/shard_map/all_gather | solution.py:135
  38.6 9.4 all_gather.36
  49.5 3.5 fusion.77
  58.4 5.6 copy.50
  64.0 5.1 fusion.58
  70.3 17.2 %fusion.15 = (f32[6,3,512]{2,1,0:T(4,128)S(1)}, f32[6,1024,512,3]{2,1,3,0:T(8,128)}) fusion(pred[512,1024]{0,1:T(8,128)(4,1)S(1)} %get-tuple-element.47, bf16[1,1024,6,3,64]{1,4,3,2,0:T(8,128)(2,1)S(1)} %bitcast.337, bf16[1024,6,32]{0,2,1:T(8,128)(2,1)S(1)} %copy-done.14, bf16[1024,6,32]{0,2,1:T(8,128)(2,1)S(1)} %copy-done.13), kind=kOutput, calls=%fused_computation.29 | convolution fusion | flops 1237834752 | bytes 40275968 | tf_op jit(solution)/shard_map/qgrd,kgd->grqk/dot_general | solution.py:67
  87.6 15.3 %fusion.14 = (f32[6,3,512]{2,1,0:T(4,128)S(1)}, f32[6,1024,512,3]{2,1,3,0:T(8,128)}) fusion(pred[512,1024]{0,1:T(8,128)(4,1)S(1)} %get-tuple-element.46, bf16[1,1024,6,3,64]{1,4,3,2,0:T(8,128)(2,1)S(1)} %bitcast.338, bf16[1024,6,32]{0,2,1:T(8,128)(2,1)S(1)} %copy-done.14, bf16[1024,6,32]{0,2,1:T(8,128)(2,1)S(1)} %copy-done.13), kind=kOutput, calls=%fused_computation.28 | convolution fusion | flops 1237834752 | bytes 40275968 | tf_op jit(solution)/shard_map/qgrd,kgd->grqk/dot_general | solution.py:67
  102.9 36.3 %fusion.10 = (f32[6,3]{1,0:T(8,128)}, f32[6,3,512]{2,1,0:T(4,128)S(1)}, f32[6,3,512]{2,1,0:T(4,128)S(1)}, f32[6,3]{1,0:T(8,128)}) fusion(f32[6,1024,512,3]{2,1,3,0:T(8,128)} %get-tuple-element.54, pred[512,1024]{0,1:T(8,128)(4,1)S(1)} %get-tuple-element.47, f32[6,3,512]{2,1,0:T(4,128)S(1)} %get-tuple-element.53, f32[6,3,512]{2,1,0:T(4,128)S(1)} %get-tuple-element.55, ...), kind=kLoop, calls=%fused_computation.17 | loop fusion | flops 113227744 | bytes 76693648 | tf_op jit(solution)/shard_map/reduce_max | solution.py:70
  139.2 17.0 %fusion.80 = bf16[512,6,3,64]{0,3,2,1:T(8,128)(2,1)} fusion(bf16[1024,6,64,1]{0,2,3,1:T(8,128)(2,1)S(1)} %bitcast.348, f32[6,1024,512,3]{2,1,3,0:T(8,128)} %get-tuple-element.56, f32[6,3,512]{2,1,0:T(4,128)S(1)} %get-tuple-element.61, f32[6,3,512]{2,1,0:T(4,128)S(1)} %get-tuple-element.55, pred[512,1024]{0,1:T(8,128)(4,1)S(1)} %get-tuple-element.46), kind=kOutput, calls=%fused_computation.124 | convolution fusion | flops 1255735296 | bytes 40312832 | tf_op jit(solution)/shard_map/grqk,kgd->qgrd/dot_general | solution.py:76
  156.2 17.3 %fusion.81 = bf16[512,6,3,64]{0,3,2,1:T(8,128)(2,1)} fusion(bf16[1024,6,64,1]{0,2,3,1:T(8,128)(2,1)S(1)} %bitcast.349, f32[6,1024,512,3]{2,1,3,0:T(8,128)} %get-tuple-element.54, f32[6,3,512]{2,1,0:T(4,128)S(1)} %get-tuple-element.17, f32[6,3,512]{2,1,0:T(4,128)S(1)} %get-tuple-element.53, pred[512,1024]{0,1:T(8,128)(4,1)S(1)} %get-tuple-element.47), kind=kOutput, calls=%fused_computation.125 | convolution fusion | flops 1255735296 | bytes 40312832 | tf_op jit(solution)/shard_map/grqk,kgd->qgrd/dot_general | solution.py:76
  173.4 3.6 pad_maximum_fusion.2
  177.0 6.6 multiply_reduce_fusion.2
  187.8 13.2 fusion.122
  201.0 14.0 %fusion.121 = f32[1024,3072]{1,0:T(8,128)} fusion(bf16[1024,1152]{1,0:T(8,128)(2,1)} %copy-done.26, bf16[1152,3072]{1,0:T(8,128)(2,1)} %all-gather.10.cloned.1.call-done), kind=kOutput, calls=%fused_computation.183 | convolution fusion | flops 7247757312 | bytes 22020096 | tf_op jit(solution)/shard_map/dot_general | solution.py:50
  215.0 12.3 all-gather.14.cloned.1.call-done
  227.3 22.2 %multiply_convert_fusion = (bf16[1024,3072]{1,0:T(8,128)(2,1)}, bf16[1024,3072]{1,0:T(8,128)(2,1)}, bf16[1024,3072]{1,0:T(8,128)(2,1)}) fusion(f32[1024,3072]{1,0:T(8,128)} %fusion.121, f32[1024,3072]{1,0:T(8,128)} %fusion.122, bf16[3072,1152]{1,0:T(8,128)(2,1)} %all-gather.14.cloned.1.call-done, bf16[1,1024,1152]{2,1,0:T(8,128)(2,1)S(1)} %copy-done.24), kind=kOutput, calls=%fused_computation.40 | convolution fusion | flops 7294943232 | bytes 53477376 | tf_op jit(solution)/shard_map/dot_general | solution.py:60
  249.5 14.0 %fusion.123 = f32[1024,1152]{1,0:T(8,128)} fusion(bf16[1024,3072]{1,0:T(8,128)(2,1)} %get-tuple-element.36, bf16[1152,3072]{1,0:T(8,128)(2,1)} %all-gather.10.cloned.1.call-done), kind=kOutput, calls=%fused_computation.185 | convolution fusion | flops 7247757312 | bytes 18087936 | tf_op jit(solution)/shard_map/dot_general | solution.py:60
  263.5 15.8 %multiply_reduce_fusion = (bf16[1152]{0:T(1024)(128)(2,1)}, f32[1024]{0:T(1024)S(1)}, f32[1024,1152]{1,0:T(8,128)S(1)}) fusion(f32[1024,1152]{1,0:T(8,128)} %copy-done.4, f32[1024]{0:T(1024)S(1)} %add_rsqrt_fusion, f32[1152]{0:T(1024)S(1)} %copy-done.40, f32[1024,1152]{1,0:T(8,128)} %fusion.123, bf16[1024,3072]{1,0:T(8,128)(2,1)} %get-tuple-element.35, ...), kind=kOutput, calls=%fused_computation.79 | convolution fusion | flops 7256012800 | bytes 27540224 | tf_op jit(solution)/shard_map/dot_general | solution.py:60
  280.8 2.2 copy-done.3
  283.0 5.0 convolution_convert_fusion.5
  288.0 2.9 copy.53
  290.9 14.7 %fusion.87 = f32[6,1024,512,3]{2,1,3,0:T(8,128)} fusion(bf16[1024,6,64,1]{0,2,3,1:T(8,128)(2,1)S(1)} %bitcast.350, bf16[1,1024,6,3,64]{1,4,3,2,0:T(8,128)(2,1)S(1)} %bitcast.341), kind=kOutput, calls=%fused_computation.136 | convolution fusion | flops 1207959552 | bytes 39714816 | tf_op jit(solution)/shard_map/qgrd,kgd->grqk/dot_general | solution.py:90
  305.6 14.7 %fusion.86 = f32[6,1024,512,3]{2,1,3,0:T(8,128)} fusion(bf16[1024,6,64,1]{0,2,3,1:T(8,128)(2,1)S(1)} %bitcast.351, bf16[1,1024,6,3,64]{1,4,3,2,0:T(8,128)(2,1)S(1)} %bitcast.342), kind=kOutput, calls=%fused_computation.135 | convolution fusion | flops 1207959552 | bytes 39714816 | tf_op jit(solution)/shard_map/qgrd,kgd->grqk/dot_general | solution.py:90
  320.3 15.9 %fusion.20 = f32[6,64,1024,1]{2,1,3,0:T(8,128)} fusion(f32[6,1024,512,3]{2,1,3,0:T(8,128)} %get-tuple-element.54, f32[6,3,512]{2,1,0:T(4,128)S(1)} %copy-done.43, pred[512,1024]{0,1:T(8,128)(4,1)S(1)} %copy-done.10, bf16[1,1024,6,3,64]{1,4,3,2,0:T(8,128)(2,1)S(1)} %bitcast.343), kind=kOutput, calls=%fused_computation.34 | convolution fusion | flops 1245708288 | bytes 41074688 | tf_op jit(solution)/shard_map/grqk,qgrd->kgd/dot_general | solution.py:101
  336.2 16.7 %fusion.71 = bf16[6,64,1024]{2,1,0:T(8,128)(2,1)S(1)} fusion(f32[6,64,1024,1]{2,1,3,0:T(8,128)} %fusion.20, f32[6,1024,512,3]{2,1,3,0:T(8,128)} %get-tuple-element.56, f32[6,3,512]{2,1,0:T(4,128)S(1)} %copy-done.42, pred[512,1024]{0,1:T(8,128)(4,1)S(1)} %copy-done.8, bf16[1,1024,6,3,64]{1,4,3,2,0:T(8,128)(2,1)} %bitcast.344), kind=kOutput, calls=%fused_computation.118 | convolution fusion | flops 1246494720 | bytes 41848832 | tf_op jit(solution)/shard_map/grqk,qgrd->kgd/dot_general | solution.py:101
  353.8 2.6 convolution_convert_fusion.6
  356.5 50.9 %fusion.30 = f32[6,64,1024,1]{2,1,3,0:T(8,128)} fusion(f32[6,1024,512,3]{2,1,3,0:T(8,128)} %fusion.86, f32[6,1024,512,3]{2,1,3,0:T(8,128)} %get-tuple-element.56, f32[6,3,512]{2,1,0:T(4,128)S(1)} %copy-done.42, pred[512,1024]{0,1:T(8,128)(4,1)S(1)} %copy-done.8, bf16[1,1024,6,3,64]{1,4,3,2,0:T(8,128)(2,1)} %bitcast.339), kind=kOutput, calls=%fused_computation.51 | convolution fusion | flops 1311778816 | bytes 154894336 | tf_op jit(solution)/shard_map/grqk,qgrd->kgd/dot_general | solution.py:98
  407.4 51.7 %fusion.72 = f32[1024,6,64]{0,2,1:T(8,128)} fusion(f32[6,64,1024,1]{2,1,3,0:T(8,128)} %fusion.30, f32[6,1024,512,3]{2,1,3,0:T(8,128)} %fusion.87, f32[6,1024,512,3]{2,1,3,0:T(8,128)} %get-tuple-element.54, f32[6,3,512]{2,1,0:T(4,128)} %log_add_fusion, pred[512,1024]{0,1:T(8,128)(4,1)S(1)} %copy-done.10, bf16[1,1024,6,3,64]{1,4,3,2,0:T(8,128)(2,1)} %bitcast.340), kind=kOutput, calls=%fused_computation.120 | convolution fusion | flops 1312172032 | bytes 156467200 | tf_op jit(solution)/shard_map/grqk,qgrd->kgd/dot_general | solution.py:98
  459.1 1.6 multiply_subtract_fusion.1
  461.7 2.6 convolution_convert_fusion.7
  464.6 7.8 convolution_convert_fusion.3
  472.4 52.2 %fusion.69 = f32[512,6,3,64]{0,3,2,1:T(8,128)} fusion(f32[6,1024,512,3]{2,1,3,0:T(8,128)} %fusion.87, f32[6,1024,512,3]{2,1,3,0:T(8,128)} %get-tuple-element.54, f32[6,3,512]{2,1,0:T(4,128)} %log_add_fusion, pred[512,1024]{0,1:T(8,128)(4,1)S(1)} %copy-done.10, bf16[1024,6,32]{0,2,1:T(8,128)(2,1)} %get-tuple-element.45, ...), kind=kOutput, calls=%fused_computation.114 | convolution fusion | flops 1313351680 | bytes 79204352 | tf_op jit(solution)/shard_map/grqk,kgd->qgrd/dot_general | solution.py:95
  524.7 50.5 %fusion.70 = f32[512,6,3,64]{0,3,2,1:T(8,128)} fusion(f32[6,1024,512,3]{2,1,3,0:T(8,128)} %fusion.86, f32[6,1024,512,3]{2,1,3,0:T(8,128)} %get-tuple-element.56, f32[6,3,512]{2,1,0:T(4,128)} %log_add_fusion.1, pred[512,1024]{0,1:T(8,128)(4,1)S(1)} %copy-done.8, bf16[1024,6,32]{0,2,1:T(8,128)(2,1)} %get-tuple-element.45, ...), kind=kOutput, calls=%fused_computation.115 | convolution fusion | flops 1313351680 | bytes 79204352 | tf_op jit(solution)/shard_map/grqk,kgd->qgrd/dot_general | solution.py:95
  575.2 2.8 pad_maximum_fusion
  580.4 5.1 convolution_convert_fusion.4
  585.6 13.0 convolution_convert_fusion
  598.7 12.7 convolution_convert_fusion.2
  611.5 12.3 convolution_convert_fusion.1
  625.2 40.1 %pmax.7 = f32[18]{0:T(128)S(1)} all-reduce(f32[18]{0:T(128)S(1)} %max.20), channel_id=1, replica_groups=mesh['rep'=8,'shard'=4] {'rep','shard'}, use_global_device_ids=true, to_apply=%region_34.35 | all-reduce | flops 18 | bytes 144 | tf_op jit(solution)/shard_map/pmax | solution.py:171
  667.7 6.3 fusion.124
  675.6 4.1 fusion.48
  679.7 6.8 all-reduce.5
  686.8 6.0 fusion.47
  692.7 15.3 %fusion.52 = bf16[1,1024,1152]{2,1,0:T(8,128)(2,1)} fusion(f32[1024,1152]{1,0:T(8,128)} %copy-done.4, bf16[1024,3072]{1,0:T(8,128)(2,1)} %get-tuple-element.37, bf16[3072,1152]{1,0:T(8,128)(2,1)} %all-gather.14.cloned.1.call-done), kind=kOutput, calls=%fused_computation.87 | convolution fusion | flops 7250116608 | bytes 20447232 | tf_op jit(solution)/shard_map/dot_general | solution.py:50
  708.1 46.1 %reduce-scatter.16.cloned.1.call-done = bf16[288,3072]{1,0:T(8,128)(2,1)} async-done(((bf16[1152,3072]{1,0:T(8,128)(2,1)}), bf16[288,3072]{1,0:T(8,128)(2,1)}) %reduce-scatter.16.cloned.1.call-update) | async-done | bytes 1769488 | tf_op jit(solution)/shard_map/reduce_scatter | solution.py:221
  754.2 66.0 %reduce-scatter.18.cloned.1.call-done = bf16[288,3072]{1,0:T(8,128)(2,1)} async-done(((bf16[1152,3072]{1,0:T(8,128)(2,1)}), bf16[288,3072]{1,0:T(8,128)(2,1)}) %reduce-scatter.18.cloned.1.call-update) | async-done | bytes 1769488 | tf_op jit(solution)/shard_map/reduce_scatter | solution.py:224
  820.3 547.2 %all-reduce.8 = (f32[288,1152]{1,0:T(8,128)}, f32[288,384]{1,0:T(8,128)}, f32[288,384]{1,0:T(8,128)}, f32[288,1152]{1,0:T(8,128)}, f32[288,3072]{1,0:T(8,128)}, ...) all-reduce(bf16[288,1152]{1,0:T(8,128)(2,1)} %reduce-scatter.8.clon, ...), channel_id=1, replica_groups=mesh['rep'=8,'shard'=4] {'rep'}, use_global_device_ids=true, to_apply=%region_13.14 | all-reduce | flops 3539520 | bytes 21238272 | tf_op jit(solution)/shard_map/psum | solution.py:311
  (208 shorter events, 31.0 us)
Async XLA Ops:
  7.2 5.6 copy-start.51
  7.2 6.8 copy-start.52
  7.2 7.0 copy-start.53
  7.2 17.0 %copy-start.35 = (bf16[288,384]{1,0:T(8,128)(2,1)S(1)}, bf16[288,384]{1,0:T(8,128)(2,1)}, u32[]{:S(2)}) copy-start(bf16[288,384]{1,0:T(8,128)(2,1)} %param.16) | copy-start | bytes 663556
  7.2 51.2 %all-gather.6.cloned.1.call-start = ((), (), s32[]{:S(2)}) async-start(), calls=%async_computation.7 | async-start | bytes 3317760 | tf_op jit(solution)/shard_map/all_gather | solution.py:133
  8.0 30.6 %copy-start.31 = (bf16[288,384]{1,0:T(8,128)(2,1)S(1)}, bf16[288,384]{1,0:T(8,128)(2,1)}, u32[]{:S(2)}) copy-start(bf16[288,384]{1,0:T(8,128)(2,1)} %param.15) | copy-start | bytes 663556
  8.0 169.0 %all-gather.8.cloned.1.call-start = ((), (), s32[]{:S(2)}) async-start(), calls=%async_computation.8 | async-start | bytes 3317760 | tf_op jit(solution)/shard_map/all_gather | solution.py:136
  8.7 177.7 %all-gather.12.cloned.1.call-start = ((), (), s32[]{:S(2)}) async-start(), calls=%async_computation.10 | async-start | bytes 8847360 | tf_op jit(solution)/shard_map/all_gather | solution.py:178
  9.5 191.5 %all-gather.10.cloned.1.call-start = ((), (), s32[]{:S(2)}) async-start(), calls=%async_computation.9 | async-start | bytes 8847360 | tf_op jit(solution)/shard_map/all_gather | solution.py:177
  10.1 217.3 %all-gather.14.cloned.1.call-start = ((), (), s32[]{:S(2)}) async-start(), calls=%async_computation.11 | async-start | bytes 8847360 | tf_op jit(solution)/shard_map/all_gather | solution.py:179
  10.6 697.4 %reduce-scatter.12.cloned.1.call-start = ((), (), s32[]{:S(2)}) async-start(), calls=%async_computation.14 | async-start | bytes 1105920 | tf_op jit(solution)/shard_map/reduce_scatter | solution.py:301
  12.7 51.3 %copy-start.44 = (f32[1024]{0:T(1024)}, f32[1024]{0:T(1024)S(1)}, u32[]{:S(2)}) copy-start(f32[1024]{0:T(1024)S(1)} %add_rsqrt_fusion.1) | copy-start | bytes 12292
  23.0 41.0 %copy-start.38 = (f32[1152]{0:T(1024)}, f32[1152]{0:T(1024)S(1)}, u32[]{:S(2)}) copy-start(f32[1152]{0:T(1024)S(1)} %convert_element_type.200) | copy-start | bytes 13828
  23.6 29.4 %copy-start.48 = (s32[1024]{0:T(1024)}, s32[1024]{0:T(1024)S(1)}, u32[]{:S(2)}) copy-start(s32[1024]{0:T(1024)S(1)} %iota.31) | copy-start | bytes 12292
  48.0 6.4 copy-start.11
  56.3 12.9 copy-start.16
  58.4 80.8 %copy-start.7 = (pred[512,1024]{0,1:T(8,128)(4,1)}, pred[512,1024]{0,1:T(8,128)(4,1)S(1)}, u32[]{:S(2)}) copy-start(pred[512,1024]{0,1:T(8,128)(4,1)S(1)} %get-tuple-element.46) | copy-start | bytes 1572868
  58.4 97.8 %copy-start.9 = (pred[512,1024]{0,1:T(8,128)(4,1)}, pred[512,1024]{0,1:T(8,128)(4,1)S(1)}, u32[]{:S(2)}) copy-start(pred[512,1024]{0,1:T(8,128)(4,1)S(1)} %get-tuple-element.47) | copy-start | bytes 1572868
  64.0 5.2 copy-start.29
  70.3 17.3 %copy-start.5 = (bf16[1024,18,64]{0,2,1:T(8,128)(2,1)}, bf16[1024,18,64]{0,2,1:T(8,128)(2,1)S(1)}, u32[]{:S(2)}) copy-start(bf16[1024,18,64]{0,2,1:T(8,128)(2,1)S(1)} %pad_maximum_fusion.1) | copy-start | bytes 7077892
  102.9 36.3 %copy-start.20 = (bf16[1024,384]{0,1:T(8,128)(2,1)S(1)}, bf16[1024,384]{0,1:T(8,128)(2,1)}, u32[]{:S(2)}) copy-start(bf16[1024,384]{0,1:T(8,128)(2,1)} %fusion.77) | copy-start | bytes 2359300
  139.2 17.0 %copy-start.36 = (f32[6,3,512]{2,1,0:T(4,128)}, f32[6,3,512]{2,1,0:T(4,128)S(1)}, u32[]{:S(2)}) copy-start(f32[6,3,512]{2,1,0:T(4,128)S(1)} %get-tuple-element.17) | copy-start | bytes 110596
  177.0 6.6 copy-start.37
  177.0 8.9 copy-start.40
  201.0 26.3 %copy-start.24 = (bf16[1,1024,1152]{2,1,0:T(8,128)(2,1)S(1)}, bf16[1,1024,1152]{2,1,0:T(8,128)(2,1)}, u32[]{:S(2)}) copy-start(bf16[1,1024,1152]{2,1,0:T(8,128)(2,1)} %param.23) | copy-start | bytes 7077892
  249.5 29.9 %slice-start = ((s8[4718592]{0:T(1024)(128)(4,1)}), s8[4194304]{0:T(1024)(128)(4,1)S(1)}, s32[]{:S(2)}) async-start(s8[4718592]{0:T(1024)(128)(4,1)} %bitcast.334), calls=%async_computation.19 | async-start | bytes 8388608
  263.5 15.9 %slice-start.1 = ((s8[4718592]{0:T(1024)(128)(4,1)}), s8[524288]{0:T(1024)(128)(4,1)S(1)}, s32[]{:S(2)}) async-start(s8[4718592]{0:T(1024)(128)(4,1)} %bitcast.334), calls=%async_computation.20 | async-start | bytes 1048576
  290.9 29.4 %copy-start.6 = (bf16[1024,1152]{0,1:T(8,128)(2,1)}, bf16[1024,1152]{0,1:T(8,128)(2,1)S(1)}, u32[]{:S(2)}) copy-start(bf16[1024,1152]{0,1:T(8,128)(2,1)S(1)} %copy.53) | copy-start | bytes 7077892
  290.9 14.7 %copy-start.22 = (bf16[1024,384]{0,1:T(8,128)(2,1)S(1)}, bf16[1024,384]{0,1:T(8,128)(2,1)}, u32[]{:S(2)}) copy-start(bf16[1024,384]{0,1:T(8,128)(2,1)} %fusion.77) | copy-start | bytes 2359300
  305.6 14.7 %copy-start.10 = (pred[512,1024]{0,1:T(8,128)(4,1)S(1)}, pred[512,1024]{0,1:T(8,128)(4,1)}, u32[]{:S(2)}) copy-start(pred[512,1024]{0,1:T(8,128)(4,1)} %copy-done.9) | copy-start | bytes 1572868
  305.6 14.7 %copy-start.43 = (f32[6,3,512]{2,1,0:T(4,128)S(1)}, f32[6,3,512]{2,1,0:T(4,128)}, u32[]{:S(2)}) copy-start(f32[6,3,512]{2,1,0:T(4,128)} %log_add_fusion) | copy-start | bytes 110596
  320.3 15.9 %copy-start.8 = (pred[512,1024]{0,1:T(8,128)(4,1)S(1)}, pred[512,1024]{0,1:T(8,128)(4,1)}, u32[]{:S(2)}) copy-start(pred[512,1024]{0,1:T(8,128)(4,1)} %copy-done.7) | copy-start | bytes 1572868
  320.3 15.9 %copy-start.42 = (f32[6,3,512]{2,1,0:T(4,128)S(1)}, f32[6,3,512]{2,1,0:T(4,128)}, u32[]{:S(2)}) copy-start(f32[6,3,512]{2,1,0:T(4,128)} %log_add_fusion.1) | copy-start | bytes 110596
  336.2 17.6 %copy-start.2 = (bf16[1,1024,1152]{2,1,0:T(8,128)(2,1)S(1)}, bf16[1,1024,1152]{2,1,0:T(8,128)(2,1)}, u32[]{:S(2)}) copy-start(bf16[1,1024,1152]{2,1,0:T(8,128)(2,1)} %param.12) | copy-start | bytes 7077892
  336.2 17.6 %copy-start.39 = (f32[1152]{0:T(1024)S(1)}, f32[1152]{0:T(1024)}, u32[]{:S(2)}) copy-start(f32[1152]{0:T(1024)} %copy-done.38) | copy-start | bytes 13828
  336.2 17.6 %copy-start.45 = (f32[1024]{0:T(1024)S(1)}, f32[1024]{0:T(1024)}, u32[]{:S(2)}) copy-start(f32[1024]{0:T(1024)} %copy-done.44) | copy-start | bytes 12292
  356.4 351.6 %reduce-scatter.10.cloned.1.call-start = ((), (), s32[]{:S(2)}) async-start(), calls=%async_computation.13 | async-start | bytes 1105920 | tf_op jit(solution)/shard_map/reduce_scatter | solution.py:298
  407.4 51.7 %copy-start.17 = (f32[1024,32]{0,1:T(8,128)S(1)}, f32[1024,32]{0,1:T(8,128)}, u32[]{:S(2)}) copy-start(f32[1024,32]{0,1:T(8,128)} %copy-done.16) | copy-start | bytes 393220
  464.4 243.7 %reduce-scatter.14.cloned.1.call-start = ((), (), s32[]{:S(2)}) async-start(), calls=%async_computation.15 | async-start | bytes 3317760 | tf_op jit(solution)/shard_map/reduce_scatter | solution.py:304
  472.4 235.7 %reduce-scatter.8.cloned.1.call-start = ((), (), s32[]{:S(2)}) async-start(), calls=%async_computation.12 | async-start | bytes 3317760 | tf_op jit(solution)/shard_map/reduce_scatter | solution.py:295
  585.5 122.6 %reduce-scatter.20.cloned.1.call-start = ((), (), s32[]{:S(2)}) async-start(), calls=%async_computation.18 | async-start | bytes 8847360 | tf_op jit(solution)/shard_map/reduce_scatter | solution.py:227
  598.6 155.6 %reduce-scatter.16.cloned.1.call-start = ((), (), s32[]{:S(2)}) async-start(), calls=%async_computation.16 | async-start | bytes 8847360 | tf_op jit(solution)/shard_map/reduce_scatter | solution.py:221
  611.4 208.9 %reduce-scatter.18.cloned.1.call-start = ((), (), s32[]{:S(2)}) async-start(), calls=%async_computation.17 | async-start | bytes 8847360 | tf_op jit(solution)/shard_map/reduce_scatter | solution.py:224
  623.8 42.0 %copy-start.32 = (bf16[288,384]{1,0:T(8,128)(2,1)S(1)}, bf16[288,384]{1,0:T(8,128)(2,1)}, u32[]{:S(2)}) copy-start(bf16[288,384]{1,0:T(8,128)(2,1)} %param.15) | copy-start | bytes 663556
  623.8 42.8 %copy-start.23 = (bf16[288,1152]{1,0:T(8,128)(2,1)S(1)}, bf16[288,1152]{1,0:T(8,128)(2,1)}, u32[]{:S(2)}) copy-start(bf16[288,1152]{1,0:T(8,128)(2,1)} %param.14) | copy-start | bytes 1990660
  665.2 8.8 copy-start.55
  667.7 6.3 copy-start.12
  667.7 6.3 copy-start.19
  (24 other events, 57.3 us)
Sparse Core Ops, SparseCore 0:
  9.6 33.2 all-gather.5
  44.5 25.7 all-gather.7
  71.8 50.8 all-gather.11
  124.1 50.8 all-gather.9
  176.4 50.8 all-gather.13
  356.6 23.8 reduce-scatter.11
  464.5 23.8 reduce-scatter.9
  491.5 34.8 reduce-scatter.13
  585.7 35.0 reduce-scatter.7
  623.2 64.5 reduce-scatter.19
  690.5 63.6 reduce-scatter.15
  756.6 63.6 reduce-scatter.17
where the time goes:
time: 1380 us; the launch traced here: 1370 us
  blocking collectives  626 us (45%)
  matrix products  518 us (38%)
  waiting for transfers between devices  128 us (9%)
  other arithmetic  64.7 us (5%)
  local copies, waits for them, and re-layouts  20.4 us (1%)
  between operations  16.5 us (1%)
    psum x1, blocking collectives, on_device(): lax.psum((attention_sums[0], attention_sums[1], attention_sums[2], attent...  547 us
    dot_general x2, matrix products, attend_backward(): jnp.einsum('grqk,kgd->qgrd', grad_scores, key_heads, preferred_element_ty...  103 us
    dot_general x2, matrix products, attend_backward(): jnp.einsum('grqk,qgrd->kgd', grad_scores, query_block, preferred_element_...  103 us
    dot_general x7, matrix products, product_right(): lax.dot_general(left, right, (((1,), (1,)), ((), ())), preferred_element_...  69 us
    reduce_scatter x1, waiting for transfers between devices, on_device(): lax.psum_scatter(up_term.astype(jnp.bfloat16), 'shard', scatter_dimension...  66 us
    dot_general x7, matrix products, product(): return jnp.dot(left, right, preferred_element_type=jnp.float32)  59.2 us
    dot_general x7, matrix products, product_left(): lax.dot_general(left, right, (((0,), (0,)), ((), ())), preferred_element_...  56.1 us
    reduce_scatter x1, waiting for transfers between devices, on_device(): lax.psum_scatter(gate_term.astype(jnp.bfloat16), 'shard', scatter_dimensi...  46.1 us
  transfers between devices with their start and end apart: 12, of which 3 were waited for; matrix products, arithmetic and copies ran while one was open for 34% of the time, Pallas kernels for 0%

commit v1 on v0

v1 whole, which is shorter than its diff:
```python
import functools
import math

import jax
import jax.numpy as jnp
from jax import lax
from jax.experimental import pallas as pl
from jax.experimental.pallas import tpu as pltpu
from jax.sharding import PartitionSpec as P

HEADS = 18
KV_HEADS = 6
MOST_DOC = 512
eps_norm = 1e-05
rope_base = 10000.0
clip_tau = 2.5
HEAD_DIM = 64
TQ = 128
f32 = jnp.float32
bf16 = jnp.bfloat16
NT = (((1,), (1,)), ((), ()))
NN = (((1,), (0,)), ((), ()))
TN = (((0,), (0,)), ((), ()))


def dot(a, b, dims):
    return lax.dot_general(a, b, dims, preferred_element_type=f32)


def doubled(tile, half):
    low = lax.broadcasted_iota(jnp.int32, tile.shape, 1) < HEAD_DIM
    other = pltpu.roll(tile.astype(f32), HEAD_DIM, 1).astype(tile.dtype)
    return jnp.where(low, tile, other) if half == 0 else jnp.where(low, other, tile)


def stack_heads(tiles, kv_half):
    low = lax.broadcasted_iota(jnp.int32, (TQ, 128), 1) < HEAD_DIM
    parts = []
    for a in range(3 * kv_half, 3 * kv_half + 3):
        t = tiles[:, (a // 2) * 128 : (a // 2) * 128 + 128]
        zero = jnp.zeros_like(t)
        parts.append(jnp.where(low, t, zero) if a % 2 == 0 else jnp.where(low, zero, t))
    return jnp.concatenate(parts, axis=0)


def forward_kernel(first_ref, q_ref, k_ref, v_ref, start_ref, out_ref, top_ref, kd, vd, *, most):
    g, i = pl.program_id(0), pl.program_id(1)

    @pl.when(i == 0)
    def _():
        for half in range(2):
            kd[half] = doubled(k_ref[...], half)
            vd[half] = doubled(v_ref[...], half)

    first = first_ref[i]
    count = i + 1 - first
    for width in range(1, most + 1):

        @pl.when(count == width)
        def _(width=width):
            span = width * TQ
            base = pl.multiple_of(first * TQ, TQ)
            row = lax.broadcasted_iota(jnp.int32, (TQ, span), 0) + i * TQ
            col = lax.broadcasted_iota(jnp.int32, (TQ, span), 1) + base
            bias = jnp.where((col <= row) & (col >= start_ref[...]), 0.0, -1e30)
            low = lax.broadcasted_iota(jnp.int32, (TQ, 128), 1) < HEAD_DIM
            tiles = q_ref[...]
            heads = []
            for half in range(2):
                keys = kd[half, pl.ds(base, span), :]
                vals = vd[half, pl.ds(base, span), :]
                s = dot(stack_heads(tiles, half), keys, NT)
                weights, scales = [], []
                for n in range(3):
                    sn = s[n * TQ : n * TQ + TQ] * 0.125 + bias
                    peak = jnp.max(sn, axis=1, keepdims=True)
                    e = jnp.exp(sn - peak)
                    total = jnp.sum(e, axis=1, keepdims=True)
                    a = 3 * half + n
                    top_ref[a] = jnp.broadcast_to(jnp.max(peak, axis=0, keepdims=True), (8, 128))
                    weights.append(e.astype(bf16))
                    scales.append(1.0 / total)
                o = dot(jnp.concatenate(weights, axis=0), vals, NN)
                for n in range(3):
                    heads.append(o[n * TQ : n * TQ + TQ] * scales[n])
            for t in range(3):
                out_ref[:, t * 128 : t * 128 + 128] = jnp.where(low, heads[2 * t], heads[2 * t + 1]).astype(bf16)


def attention_forward(q, k, v, start_col, first, most):
    length = q.shape[0]
    pairs = k.shape[1] // 128
    blocks = length // TQ
    mixed, tops = pl.pallas_call(
        functools.partial(forward_kernel, most=most),
        grid_spec=pltpu.PrefetchScalarGridSpec(
            num_scalar_prefetch=1,
            grid=(pairs, blocks),
            in_specs=[
                pl.BlockSpec((TQ, 384), lambda g, i, s: (i, g)),
                pl.BlockSpec((length, 128), lambda g, i, s: (0, g)),
                pl.BlockSpec((length, 128), lambda g, i, s: (0, g)),
                pl.BlockSpec((TQ, 1), lambda g, i, s: (i, 0)),
            ],
            out_specs=[
                pl.BlockSpec((TQ, 384), lambda g, i, s: (i, g)),
                pl.BlockSpec((None, None, 6, 8, 128), lambda g, i, s: (i, g, 0, 0, 0)),
            ],
            scratch_shapes=[pltpu.VMEM((2, length, 128), bf16), pltpu.VMEM((2, length, 128), bf16)],
        ),
        out_shape=[
            jax.ShapeDtypeStruct(q.shape, bf16),
            jax.ShapeDtypeStruct((blocks, pairs, 6, 8, 128), f32),
        ],
        name="attention_forward",
    )(first, q, k, v, start_col)
    return mixed, jnp.max(tops[:, :, :, 0, 0], axis=0).reshape(pairs * 6)


def unrotate(u, cosine, sine):
    lane = lax.broadcasted_iota(jnp.int32, u.shape, 1)
    swapped = jnp.where(lane % 64 < 32, pltpu.roll(u, 96, 1), pltpu.roll(u, 32, 1))
    return u * cosine - swapped * sine


def backward_kernel(first_ref, q_ref, k_ref, v_ref, g_ref, start_ref, cos_ref, sin_ref, cosall_ref, sinall_ref,
                    dq_ref, dk_ref, dv_ref, kd, vd, dka, dva, *, most):
    g, i = pl.program_id(0), pl.program_id(1)

    @pl.when(i == 0)
    def _():
        for half in range(2):
            kd[half] = doubled(k_ref[...], half)
            vd[half] = doubled(v_ref[...], half)
        dka[...] = jnp.zeros_like(dka)
        dva[...] = jnp.zeros_like(dva)

    first = first_ref[i]
    count = i + 1 - first
    for width in range(1, most + 1):

        @pl.when(count == width)
        def _(width=width):
            span = width * TQ
            base = pl.multiple_of(first * TQ, TQ)
            rows = pl.ds(base, span)
            col = lax.broadcasted_iota(jnp.int32, (span, TQ), 1) + i * TQ
            row = lax.broadcasted_iota(jnp.int32, (span, TQ), 0) + base
            bias = jnp.where((row <= col) & (row >= start_ref[...]), 0.0, -1e30)
            low = lax.broadcasted_iota(jnp.int32, (TQ, 128), 1) < HEAD_DIM
            q_tiles, g_tiles = q_ref[...], g_ref[...]
            heads = []
            for half in range(2):
                keys, vals = kd[half, rows, :], vd[half, rows, :]
                qs, gs = stack_heads(q_tiles, half), stack_heads(g_tiles, half)
                s = dot(keys, qs, NT)
                dp = dot(vals, gs, NT)
                probs, grads = [], []
                for n in range(3):
                    sn = s[:, n * TQ : n * TQ + TQ] * 0.125 + bias
                    peak = jnp.max(sn, axis=0, keepdims=True)
                    e = jnp.exp(sn - peak)
                    soft = e * (1.0 / jnp.sum(e, axis=0, keepdims=True))
                    dpn = dp[:, n * TQ : n * TQ + TQ]
                    inner = jnp.sum(soft * dpn, axis=0, keepdims=True)
                    probs.append(soft.astype(bf16))
                    grads.append((soft * (dpn - inner) * 0.125).astype(bf16))
                p = jnp.concatenate(probs, axis=1)
                ds = jnp.concatenate(grads, axis=1)
                dva[half, rows, :] += dot(p, gs, NN)
                dka[half, rows, :] += dot(ds, qs, NN)
                dq = dot(ds, keys, TN)
                for n in range(3):
                    heads.append(dq[n * TQ : n * TQ + TQ])
            for t in range(3):
                tile = jnp.where(low, heads[2 * t], heads[2 * t + 1])
                dq_ref[:, t * 128 : t * 128 + 128] = unrotate(tile, cos_ref[...], sin_ref[...]).astype(bf16)

    @pl.when(i == pl.num_programs(1) - 1)
    def _():
        def joined(acc):
            a, b = acc[0], acc[1]
            low = lax.broadcasted_iota(jnp.int32, a.shape, 1) < HEAD_DIM
            return jnp.where(low, a + pltpu.roll(a, HEAD_DIM, 1), b + pltpu.roll(b, HEAD_DIM, 1))

        dk_ref[...] = unrotate(joined(dka), cosall_ref[...], sinall_ref[...]).astype(bf16)
        dv_ref[...] = joined(dva).astype(bf16)


def attention_backward(q, k, v, g, start_row, cosine, sine, first, most):
    length = q.shape[0]
    pairs = k.shape[1] // 128
    blocks = length // TQ
    whole = lambda g, i, s: (0, g)
    mine = lambda g, i, s: (i, g)
    return pl.pallas_call(
        functools.partial(backward_kernel, most=most),
        grid_spec=pltpu.PrefetchScalarGridSpec(
            num_scalar_prefetch=1,
            grid=(pairs, blocks),
            in_specs=[
                pl.BlockSpec((TQ, 384), mine),
                pl.BlockSpec((length, 128), whole),
                pl.BlockSpec((length, 128), whole),
                pl.BlockSpec((TQ, 384), mine),
                pl.BlockSpec((1, TQ), lambda g, i, s: (0, i)),
                pl.BlockSpec((TQ, 128), lambda g, i, s: (i, 0)),
                pl.BlockSpec((TQ, 128), lambda g, i, s: (i, 0)),
                pl.BlockSpec((length, 128), lambda g, i, s: (0, 0)),
                pl.BlockSpec((length, 128), lambda g, i, s: (0, 0)),
            ],
            out_specs=[
                pl.BlockSpec((TQ, 384), mine),
                pl.BlockSpec((length, 128), whole),
                pl.BlockSpec((length, 128), whole),
            ],
            scratch_shapes=[pltpu.VMEM((2, length, 128), bf16), pltpu.VMEM((2, length, 128), bf16),
                            pltpu.VMEM((2, length, 128), f32), pltpu.VMEM((2, length, 128), f32)],
        ),
        out_shape=[
            jax.ShapeDtypeStruct(q.shape, bf16),
            jax.ShapeDtypeStruct(k.shape, bf16),
            jax.ShapeDtypeStruct(v.shape, bf16),
        ],
        name="attention_backward",
    )(first, q, k, v, g, start_row, cosine, sine, cosine, sine)


def project_kernel(x_ref, gain_ref, wq_ref, wk_ref, wv_ref, cos_ref, sin_ref, n_ref, q_ref, k_ref, v_ref):
    x = x_ref[...].astype(f32)
    rstd = lax.rsqrt(jnp.mean(x * x, axis=-1, keepdims=True) + eps_norm)
    normed = (x * rstd * gain_ref[...].astype(f32)).astype(bf16)
    n_ref[...] = normed
    cosine, sine = cos_ref[...], -sin_ref[...]
    for w_ref, out_ref in ((wq_ref, q_ref), (wk_ref, k_ref)):
        u = dot(normed, w_ref[...], NN)
        for t in range(out_ref.shape[1] // 128):
            lanes = slice(t * 128, t * 128 + 128)
            out_ref[:, lanes] = unrotate(u[:, lanes], cosine, sine).astype(bf16)
    v_ref[...] = dot(normed, wv_ref[...], NN).astype(bf16)


def project(x, gain, wq, wk, wv, cosine, sine):
    length, width = x.shape
    rows = 256
    row_block = lambda n: pl.BlockSpec((rows, n), lambda i: (i, 0))
    fixed = lambda a: pl.BlockSpec(a.shape, lambda i: (0, 0), pipeline_mode=pl.Buffered(1))
    return pl.pallas_call(
        project_kernel,
        grid=(length // rows,),
        in_specs=[row_block(width), fixed(gain), fixed(wq), fixed(wk), fixed(wv), row_block(128), row_block(128)],
        out_specs=[row_block(width), row_block(wq.shape[1]), row_block(wk.shape[1]), row_block(wv.shape[1])],
        out_shape=[jax.ShapeDtypeStruct((length, n), bf16) for n in (width, wq.shape[1], wk.shape[1], wv.shape[1])],
        name="project",
    )(x, gain, wq, wk, wv, cosine, sine)

def positions_of(segment_row):
    position_index = jnp.arange(segment_row.shape[0], dtype=jnp.int32)
    changed = jnp.concatenate(
        [jnp.ones((1,), dtype=jnp.bool_), segment_row[1:] != segment_row[:-1]]
    )
    starts = lax.cummax(jnp.where(changed, position_index, 0), axis=0)
    return position_index - starts


def rope_tables(places):
    half_size = HEAD_DIM // 2
    frequency = rope_base ** (-jnp.arange(half_size, dtype=jnp.float32) * 2.0 / HEAD_DIM)
    angles = places.astype(jnp.float32)[:, None] * frequency[None, :]
    cosine, sine = jnp.cos(angles), jnp.sin(angles)
    return jnp.concatenate([cosine] * 4, axis=1), jnp.concatenate([-sine, sine, -sine, sine], axis=1)


def product(left, right):
    return jnp.dot(left, right, preferred_element_type=jnp.float32)


def product_left(left, right):
    return lax.dot_general(
        left, right, (((0,), (0,)), ((), ())), preferred_element_type=jnp.float32
    )


def product_right(left, right):
    return lax.dot_general(
        left, right, (((1,), (1,)), ((), ())), preferred_element_type=jnp.float32
    )


def on_device(
    layer_input,
    segments,
    query_weight,
    key_weight,
    value_weight,
    output_weight,
    gate_weight,
    up_weight,
    down_weight,
    attention_gain,
    feedforward_gain,
    upstream,
):
    seq_count, length, model_width = layer_input.shape
    token_rows = seq_count * length
    group_size = HEADS // KV_HEADS
    query_width = HEADS * HEAD_DIM
    key_width = KV_HEADS * HEAD_DIM
    position_index = jnp.arange(length, dtype=jnp.int32)
    query_full, key_full, value_full, output_full, gain_first = (
        lax.all_gather(query_weight, "shard", axis=0, tiled=True),
        lax.all_gather(key_weight, "shard", axis=0, tiled=True),
        lax.all_gather(value_weight, "shard", axis=0, tiled=True),
        lax.all_gather(output_weight, "shard", axis=0, tiled=True),
        lax.all_gather(attention_gain, "shard", axis=0, tiled=True),
    )
    inputs = layer_input.reshape(token_rows, model_width).astype(jnp.float32)
    places = positions_of(segments[0])
    cosine, sine = rope_tables(places)
    doc_start = position_index - places
    first_block = doc_start[::TQ] // TQ
    most = min(length // TQ, MOST_DOC // TQ + 1)
    first_rstd = lax.rsqrt(jnp.mean(inputs * inputs, axis=-1, keepdims=True) + eps_norm)
    first_unit = inputs * first_rstd
    gain_first_wide = gain_first.astype(jnp.float32)
    first_normed, queries, keys_rot, values = project(
        layer_input[0], gain_first[None, :], query_full, key_full, value_full, cosine, sine
    )
    mixed, head_top = attention_forward(
        queries, keys_rot, values, doc_start[:, None], first_block, most
    )
    maxima = lax.pmax(head_top, ("rep", "shard"))
    residual = inputs + product(mixed, output_full)
    gate_full, up_full, down_full, gain_second = (
        lax.all_gather(gate_weight, "shard", axis=0, tiled=True),
        lax.all_gather(up_weight, "shard", axis=0, tiled=True),
        lax.all_gather(down_weight, "shard", axis=0, tiled=True),
        lax.all_gather(feedforward_gain, "shard", axis=0, tiled=True),
    )
    second_rstd = lax.rsqrt(jnp.mean(residual * residual, axis=-1, keepdims=True) + eps_norm)
    second_unit = residual * second_rstd
    gain_second_wide = gain_second.astype(jnp.float32)
    second_normed = (second_unit * gain_second_wide).astype(jnp.bfloat16)
    gate_values = product(second_normed, gate_full)
    up_values = product(second_normed, up_full)
    sigmoid_gate = jax.nn.sigmoid(gate_values)
    swish_gate = gate_values * sigmoid_gate
    activated = (swish_gate * up_values).astype(jnp.bfloat16)
    layer_output = (
        (residual + product(activated, down_full)).astype(jnp.bfloat16).reshape(layer_input.shape)
    )
    gate_back, up_back, down_back = (
        lax.all_gather(gate_weight, "shard", axis=0, tiled=True),
        lax.all_gather(up_weight, "shard", axis=0, tiled=True),
        lax.all_gather(down_weight, "shard", axis=0, tiled=True),
    )
    grad_output = upstream.reshape(token_rows, model_width).astype(jnp.float32)
    grad_down_in = grad_output.astype(jnp.bfloat16)
    grad_activated = product_right(grad_down_in, down_back)
    grad_gate_low = (
        grad_activated * up_values * sigmoid_gate * (1.0 + gate_values * (1.0 - sigmoid_gate))
    ).astype(jnp.bfloat16)
    grad_up_low = (grad_activated * swish_gate).astype(jnp.bfloat16)
    down_term = product_left(activated, grad_down_in)
    gate_term = product_left(second_normed, grad_gate_low)
    up_term = product_left(second_normed, grad_up_low)
    grad_second = product_right(grad_gate_low, gate_back) + product_right(grad_up_low, up_back)
    second_gain_term = jnp.sum(grad_second * second_unit, axis=0)
    grad_unit_second = grad_second * gain_second_wide
    grad_residual = (
        second_rstd
        * (
            grad_unit_second
            - second_unit * jnp.mean(grad_unit_second * second_unit, axis=-1, keepdims=True)
        )
        + grad_output
    )
    feedforward_sums = (
        lax.psum_scatter(
            gate_term.astype(jnp.bfloat16), "shard", scatter_dimension=0, tiled=True
        ),
        lax.psum_scatter(
            up_term.astype(jnp.bfloat16), "shard", scatter_dimension=0, tiled=True
        ),
        lax.psum_scatter(
            down_term.astype(jnp.bfloat16), "shard", scatter_dimension=0, tiled=True
        ),
        lax.psum_scatter(
            second_gain_term.astype(jnp.bfloat16), "shard", scatter_dimension=0, tiled=True
        ),
    )
    gate_grad, up_grad, down_grad, feedforward_gain_grad = (
        lax.psum(part, "rep").astype(jnp.float32) for part in feedforward_sums
    )
    query_back, key_back, value_back, output_back = (
        lax.all_gather(query_weight, "shard", axis=0, tiled=True),
        lax.all_gather(key_weight, "shard", axis=0, tiled=True),
        lax.all_gather(value_weight, "shard", axis=0, tiled=True),
        lax.all_gather(output_weight, "shard", axis=0, tiled=True),
    )
    grad_out_in = grad_residual.astype(jnp.bfloat16)
    output_term = product_left(mixed, grad_out_in)
    grad_mixed = product_right(grad_out_in, output_back).astype(jnp.bfloat16)
    query_low, key_low, value_low = attention_backward(
        queries, keys_rot, values, grad_mixed, doc_start[None, :], cosine, sine, first_block, most
    )
    query_term = product_left(first_normed, query_low)
    key_term = product_left(first_normed, key_low)
    value_term = product_left(first_normed, value_low)
    grad_first = (
        product_right(query_low, query_back)
        + product_right(key_low, key_back)
        + product_right(value_low, value_back)
    )
    first_gain_term = jnp.sum(grad_first * first_unit, axis=0)
    grad_unit_first = grad_first * gain_first_wide
    input_grad = (
        first_rstd
        * (
            grad_unit_first
            - first_unit * jnp.mean(grad_unit_first * first_unit, axis=-1, keepdims=True)
        )
        + grad_residual
    )
    attention_sums = (
        lax.psum_scatter(
            query_term.astype(jnp.bfloat16), "shard", scatter_dimension=0, tiled=True
        ),
        lax.psum_scatter(
            key_term.astype(jnp.bfloat16), "shard", scatter_dimension=0, tiled=True
        ),
        lax.psum_scatter(
            value_term.astype(jnp.bfloat16), "shard", scatter_dimension=0, tiled=True
        ),
        lax.psum_scatter(
            output_term.astype(jnp.bfloat16), "shard", scatter_dimension=0, tiled=True
        ),
        lax.psum_scatter(
            first_gain_term.astype(jnp.bfloat16), "shard", scatter_dimension=0, tiled=True
        ),
    )
    query_grad, key_grad, value_grad, output_grad, attention_gain_grad = (
        lax.psum(part, "rep").astype(jnp.float32) for part in attention_sums
    )
    query_factor = jnp.sqrt(clip_tau / jnp.maximum(maxima, clip_tau))
    key_factor = jnp.sqrt(
        clip_tau / jnp.maximum(jnp.max(maxima.reshape(KV_HEADS, group_size), axis=1), clip_tau)
    )
    local_rows = query_weight.shape[0]
    query_clipped = (
        query_weight.astype(jnp.float32).reshape(local_rows, HEADS, HEAD_DIM)
        * query_factor[None, :, None]
    ).reshape(local_rows, query_width)
    key_clipped = (
        key_weight.astype(jnp.float32).reshape(local_rows, KV_HEADS, HEAD_DIM)
        * key_factor[None, :, None]
    ).reshape(local_rows, key_width)
    return (
        layer_output,
        input_grad.reshape(layer_input.shape),
        query_grad,
        key_grad,
        value_grad,
        output_grad,
        gate_grad,
        up_grad,
        down_grad,
        attention_gain_grad,
        feedforward_gain_grad,
        maxima,
        query_clipped,
        key_clipped,
    )


def solution(mesh):
    return jax.shard_map(
        on_device,
        mesh=mesh,
        in_specs=(
            P(("rep", "shard"), None, None),
            P(("rep", "shard"), None),
            P("shard", None),
            P("shard", None),
            P("shard", None),
            P("shard", None),
            P("shard", None),
            P("shard", None),
            P("shard", None),
            P("shard"),
            P("shard"),
            P(("rep", "shard"), None, None),
        ),
        out_specs=(
            P(("rep", "shard"), None, None),
            P(("rep", "shard"), None, None),
            P("shard", None),
            P("shard", None),
            P("shard", None),
            P("shard", None),
            P("shard", None),
            P("shard", None),
            P("shard", None),
            P("shard"),
            P("shard"),
            P(),
            P("shard", None),
            P("shard", None),
        ),
        check_vma=False,
    )
```

time: 1380 us -> 932 us (0.68)
  blocking collectives: 626 us -> 104 us
  waiting for transfers between devices: 128 us -> 511 us
  matrix products: 518 us -> 176 us
  Pallas kernels: 0 us -> 81.1 us
  other arithmetic: 64.7 us -> 31.3 us
    psum x1, blocking collectives: 547 us -> 20.7 us  [on_device(): lax.psum(part, 'rep').astype(jnp.float32)]
    dot_general x12 -> x0, matrix products: 334 us -> none  [the longest x2 103 us: attend_backward(): jnp.einsum('grqk,kgd->qgrd', grad_scores, key_heads, preferred_element_ty...]
    psum x0 -> x1, waiting for transfers between devices: none -> 137 us  [on_device(): lax.psum(part, 'rep').astype(jnp.float32)]
    pallas_call x0 -> x3, Pallas kernels: none -> 81.1 us  [the longest x1 44.4 us: attention_backward(): pl.pallas_call(functools.partial(backward_kernel, most=most), grid_spec=p...]
    reduce_scatter x1, waiting for transfers between devices: 0.02 us -> 66.1 us  [on_device(): lax.psum_scatter(down_term.astype(jnp.bfloat16), 'shard', scatter_dimensi...]
    all_gather x1, waiting for transfers between devices: 0.02 us -> 38.7 us  [on_device(): lax.all_gather(up_weight, 'shard', axis=0, tiled=True)]
    reduce_scatter x1, waiting for transfers between devices: 0.01 us -> 38.2 us  [on_device(): lax.psum_scatter(output_term.astype(jnp.bfloat16), 'shard', scatter_dimen...]
    reduce_max x1, other arithmetic: 36.3 us -> 1.25 us  [attention_forward(): return (mixed, jnp.max(tops[:, :, :, 0, 0], axis=0).reshape(pairs * 6))]
  transfers between devices with their start and end apart: 12 -> 13, of which waited for: 3 -> 9; matrix products, arithmetic and copies ran while one was open for 34% -> 15% of each run, Pallas kernels for 0% -> 4%
where the time goes in v1:
time: 932 us; the launch traced here: 927 us
  waiting for transfers between devices  511 us (55%)
  matrix products  176 us (19%)
  blocking collectives  104 us (11%)
  Pallas kernels  81.1 us (9%)
  other arithmetic  31.3 us (3%)
  between operations  15.9 us (2%)
    psum x1, waiting for transfers between devices, on_device(): lax.psum(part, 'rep').astype(jnp.float32)  137 us
    dot_general x7, matrix products, product_right(): lax.dot_general(left, right, (((1,), (1,)), ((), ())), preferred_element_...  67.3 us
    reduce_scatter x1, waiting for transfers between devices, on_device(): lax.psum_scatter(up_term.astype(jnp.bfloat16), 'shard', scatter_dimension...  66.3 us
    reduce_scatter x1, waiting for transfers between devices, on_device(): lax.psum_scatter(gate_term.astype(jnp.bfloat16), 'shard', scatter_dimensi...  66.1 us
    reduce_scatter x1, waiting for transfers between devices, on_device(): lax.psum_scatter(down_term.astype(jnp.bfloat16), 'shard', scatter_dimensi...  66.1 us
    dot_general x7, matrix products, product_left(): lax.dot_general(left, right, (((0,), (0,)), ((), ())), preferred_element_...  60.4 us
    dot_general x4, matrix products, product(): return jnp.dot(left, right, preferred_element_type=jnp.float32)  48 us
    pallas_call x1, Pallas kernels, attention_backward(): pl.pallas_call(functools.partial(backward_kernel, most=most), grid_spec=p...  44.4 us
  transfers between devices with their start and end apart: 13, of which 9 were waited for; matrix products, arithmetic and copies ran while one was open for 15% of the time, Pallas kernels for 4%

profile of v1, /device:TPU:0, one launch (start us, length us, event | category | flops | bytes accessed | tf_op | source)
XLA Modules:
  0.0 927.1 jit_solution(1120263951624383607)
XLA Ops:
  13.1 8.5 all-reduce.7
  22.7 1.9 fusion.17
  24.6 1.9 pad_maximum_fusion
  28.5 14.1 %all_gather.36.wk_ref = bf16[1152,384]{1,0:T(8,128)(2,1)} all-gather(bf16[288,384]{1,0:T(8,128)(2,1)S(1)} %copy-done.11), channel_id=1, replica_groups=mesh['rep'=8,'shard'=4] {'shard'}, dimensions={0}, use_global_device_ids=true | all-gather | bytes 1105920 | tf_op jit(solution)/shard_map/all_gather | solution.py:312
  42.6 10.2 %all_gather.37.wv_ref = bf16[1152,384]{1,0:T(8,128)(2,1)} all-gather(bf16[288,384]{1,0:T(8,128)(2,1)S(1)} %copy-done.20), channel_id=1, replica_groups=mesh['rep'=8,'shard'=4] {'shard'}, dimensions={0}, use_global_device_ids=true | all-gather | bytes 1105920 | tf_op jit(solution)/shard_map/all_gather | solution.py:313
  52.9 10.8 %project.1 = (bf16[1024,1152]{1,0:T(8,128)(2,1)}, bf16[1024,1152]{1,0:T(8,128)(2,1)}, bf16[1024,384]{1,0:T(8,128)(2,1)}, bf16[1024,384]{1,0:T(8,128)(2,1)}) custom-call(bf16[1024,1152]{1,0:T(8,128)(2,1)} %bitcast.64, bf16[1,1152]{1,0:T(2,128)(2,1)} %broadcast_in_dim.7.gain_ref, bf16[1152,1152]{1,0:T(8,128)(2,1)} %all-gather.6.cloned.1.call-done.wq_ref, ...), custom_call_target="tpu_custom_call" | custom-call | tf_op jit(solution)/shard_map/project/pallas_call | solution.py:248
  63.7 25.8 %attention_forward.1 = (bf16[1024,1152]{1,0:T(8,128)(2,1)}, f32[8,3,6,8,128]{4,3,2,1,0:T(8,128)}) custom-call(s32[8]{0:T(128)} %and_select_fusion.first_ref, bf16[1024,1152]{1,0:T(8,128)(2,1)} %get-tuple-element.23.q_ref, bf16[1024,384]{1,0:T(8,128)(2,1)} %get-tuple-element.24.k_ref, bf16[1024,384]{1,0:T(8,128)(2,1)} %get-tuple-element.25.v_ref, ...), custom_call_target="tpu_custom_call" | custom-call | tf_op jit(solution)/shard_map/attention_forward/pallas_call | solution.py:94
  89.5 6.2 multiply_reduce_fusion.2
  95.8 2.1 copy-done.3
  98.4 24.0 %all-gather.10.cloned.1.call-done = bf16[1152,3072]{1,0:T(8,128)(2,1)} async-done(((bf16[288,3072]{1,0:T(8,128)(2,1)}), bf16[1152,3072]{1,0:T(8,128)(2,1)}) %all-gather.10.cloned.1.call-update) | async-done | bytes 7077904 | tf_op jit(solution)/shard_map/all_gather | solution.py:335
  122.4 13.6 %fusion.20 = f32[1024,3072]{1,0:T(8,128)} fusion(bf16[1024,1152]{1,0:T(8,128)(2,1)S(1)} %multiply_convert_fusion.3, bf16[1152,3072]{1,0:T(8,128)(2,1)} %all-gather.10.cloned.1.call-done), kind=kOutput, calls=%fused_computation.71 | convolution fusion | flops 7247757312 | bytes 22020096 | tf_op jit(solution)/shard_map/dot_general | solution.py:275
  136.1 38.7 %all-gather.12.cloned.1.call-done = bf16[1152,3072]{1,0:T(8,128)(2,1)} async-done(((bf16[288,3072]{1,0:T(8,128)(2,1)}), bf16[1152,3072]{1,0:T(8,128)(2,1)}) %all-gather.12.cloned.1.call-update) | async-done | bytes 7077904 | tf_op jit(solution)/shard_map/all_gather | solution.py:336
  174.7 14.0 %fusion.21 = f32[1024,3072]{1,0:T(8,128)} fusion(bf16[1024,1152]{1,0:T(8,128)(2,1)} %copy-done.8, bf16[1152,3072]{1,0:T(8,128)(2,1)} %all-gather.12.cloned.1.call-done), kind=kOutput, calls=%fused_computation.72 | convolution fusion | flops 7247757312 | bytes 22020096 | tf_op jit(solution)/shard_map/dot_general | solution.py:275
  188.7 38.3 %all-gather.14.cloned.1.call-done = bf16[3072,1152]{1,0:T(8,128)(2,1)} async-done(((bf16[768,1152]{1,0:T(8,128)(2,1)}), bf16[3072,1152]{1,0:T(8,128)(2,1)}) %all-gather.14.cloned.1.call-update) | async-done | bytes 7077904 | tf_op jit(solution)/shard_map/all_gather | solution.py:337
  227.0 22.0 %multiply_convert_fusion = (bf16[1024,3072]{1,0:T(8,128)(2,1)}, bf16[1024,3072]{1,0:T(8,128)(2,1)}, bf16[1024,3072]{1,0:T(8,128)(2,1)}) fusion(f32[1024,3072]{1,0:T(8,128)} %fusion.20, f32[1024,3072]{1,0:T(8,128)} %fusion.21, bf16[3072,1152]{1,0:T(8,128)(2,1)} %all-gather.14.cloned.1.call-done, bf16[1,1024,1152]{2,1,0:T(8,128)(2,1)S(1)} %copy-done.7), kind=kOutput, calls=%fused_computation | convolution fusion | flops 7294943232 | bytes 53477376 | tf_op jit(solution)/shard_map/dot_general | solution.py:285
  249.0 14.0 %fusion.22 = f32[1024,1152]{1,0:T(8,128)} fusion(bf16[1024,3072]{1,0:T(8,128)(2,1)} %get-tuple-element.52, bf16[1152,3072]{1,0:T(8,128)(2,1)} %all-gather.10.cloned.1.call-done), kind=kOutput, calls=%fused_computation.73 | convolution fusion | flops 7247757312 | bytes 18087936 | tf_op jit(solution)/shard_map/dot_general | solution.py:285
  263.0 15.2 %multiply_reduce_fusion = (bf16[1152]{0:T(1024)(128)(2,1)S(1)}, f32[1024]{0:T(1024)S(1)}, f32[1024,1152]{1,0:T(8,128)S(1)}) fusion(f32[1024,1152]{1,0:T(8,128)} %copy-done.3, f32[1024]{0:T(1024)S(1)} %add_rsqrt_fusion.1, f32[1152]{0:T(1024)S(1)} %convert_element_type.103, f32[1024,1152]{1,0:T(8,128)} %fusion.22, bf16[1024,3072]{1,0:T(8,128)(2,1)} %get-tuple-element.51, ...), kind=kOutput, calls=%fused_computation.25 | convolution fusion | flops 7256012800 | bytes 27540224 | tf_op jit(solution)/shard_map/dot_general | solution.py:285
  278.3 1.6 convert_add_fusion.1
  280.0 2.2 copy-done.2
  282.1 4.8 convolution_convert_fusion.5.g_ref
  286.9 44.4 %attention_backward.1 = (bf16[1024,1152]{1,0:T(8,128)(2,1)}, bf16[1024,384]{1,0:T(8,128)(2,1)}, bf16[1024,384]{1,0:T(8,128)(2,1)}) custom-call(s32[8]{0:T(128)} %and_select_fusion.first_ref, bf16[1024,1152]{1,0:T(8,128)(2,1)} %get-tuple-element.23.q_ref, bf16[1024,384]{1,0:T(8,128)(2,1)} %get-tuple-element.24.k_ref, ...), custom_call_target="tpu_custom_call" | custom-call | tf_op jit(solution)/shard_map/attention_backward/pallas_call | solution.py:196
  331.4 4.3 convolution_convert_fusion.7
  336.1 4.0 convolution_convert_fusion.6
  340.2 7.3 convolution_convert_fusion.4
  347.5 7.8 convolution_convert_fusion.3
  355.5 12.3 %convolution_convert_fusion.2 = bf16[1152,3072]{1,0:T(8,128)(2,1)} fusion(bf16[1024,1152]{1,0:T(8,128)(2,1)} %copy-done.8, bf16[1024,3072]{1,0:T(8,128)(2,1)} %get-tuple-element.52), kind=kOutput, calls=%fused_computation.7 | convolution fusion | flops 7251296256 | bytes 15728640 | tf_op jit(solution)/shard_map/dot_general | solution.py:279
  368.0 12.4 %convolution_convert_fusion.1 = bf16[1152,3072]{1,0:T(8,128)(2,1)} fusion(bf16[1024,1152]{1,0:T(8,128)(2,1)} %copy-done.8, bf16[1024,3072]{1,0:T(8,128)(2,1)} %get-tuple-element.51), kind=kOutput, calls=%fused_computation.6 | convolution fusion | flops 7251296256 | bytes 15728640 | tf_op jit(solution)/shard_map/dot_general | solution.py:279
  380.5 12.2 %convolution_convert_fusion = bf16[3072,1152]{1,0:T(8,128)(2,1)} fusion(bf16[1024,3072]{1,0:T(8,128)(2,1)} %get-tuple-element.53, bf16[1,1024,1152]{2,1,0:T(8,128)(2,1)S(1)} %copy-done.7), kind=kOutput, calls=%fused_computation.5 | convolution fusion | flops 7251296256 | bytes 15728640 | tf_op jit(solution)/shard_map/dot_general | solution.py:279
  392.9 32.9 %reduce-scatter.8.cloned.1.call-done = bf16[288,1152]{1,0:T(8,128)(2,1)} async-done(((bf16[1152,1152]{1,0:T(8,128)(2,1)}), bf16[288,1152]{1,0:T(8,128)(2,1)}) %reduce-scatter.8.cloned.1.call-update) | async-done | bytes 663568 | tf_op jit(solution)/shard_map/reduce_scatter | solution.py:426
  425.8 38.2 %reduce-scatter.14.cloned.1.call-done = bf16[288,1152]{1,0:T(8,128)(2,1)} async-done(((bf16[1152,1152]{1,0:T(8,128)(2,1)}), bf16[288,1152]{1,0:T(8,128)(2,1)}) %reduce-scatter.14.cloned.1.call-update) | async-done | bytes 663568 | tf_op jit(solution)/shard_map/reduce_scatter | solution.py:435
  464.1 66.1 %reduce-scatter.16.cloned.1.call-done = bf16[288,3072]{1,0:T(8,128)(2,1)} async-done(((bf16[1152,3072]{1,0:T(8,128)(2,1)}), bf16[288,3072]{1,0:T(8,128)(2,1)}) %reduce-scatter.16.cloned.1.call-update) | async-done | bytes 1769488 | tf_op jit(solution)/shard_map/reduce_scatter | solution.py:379
  530.2 66.3 %reduce-scatter.18.cloned.1.call-done = bf16[288,3072]{1,0:T(8,128)(2,1)} async-done(((bf16[1152,3072]{1,0:T(8,128)(2,1)}), bf16[288,3072]{1,0:T(8,128)(2,1)}) %reduce-scatter.18.cloned.1.call-update) | async-done | bytes 1769488 | tf_op jit(solution)/shard_map/reduce_scatter | solution.py:382
  596.5 66.1 %reduce-scatter.20.cloned.1.call-done = bf16[768,1152]{1,0:T(8,128)(2,1)} async-done(((bf16[3072,1152]{1,0:T(8,128)(2,1)}), bf16[768,1152]{1,0:T(8,128)(2,1)}) %reduce-scatter.20.cloned.1.call-update) | async-done | bytes 1769488 | tf_op jit(solution)/shard_map/reduce_scatter | solution.py:385
  663.3 1.2 slice_reduce_fusion
  665.3 43.1 %pmax.7 = f32[18]{0:T(128)S(1)} all-reduce(f32[18]{0:T(128)S(1)} %reshape.186), channel_id=1, replica_groups=mesh['rep'=8,'shard'=4] {'rep','shard'}, use_global_device_ids=true, to_apply=%region_27.28 | all-reduce | flops 18 | bytes 144 | tf_op jit(solution)/shard_map/pmax | solution.py:332
  709.8 1.1 convert_multiply_fusion.2
  710.9 6.4 fusion.23
  717.4 1.5 convolution_add_fusion.1
  718.9 3.4 fusion.9
  722.3 7.0 all-reduce.6
  729.5 20.7 %all-reduce.4 = (bf16[288]{0:T(512)(128)(2,1)S(1)}, bf16[288]{0:T(512)(128)(2,1)S(1)}) all-reduce(bf16[288]{0:T(512)(128)(2,1)S(1)} %dynamic-slice.3, bf16[288]{0:T(512)(128)(2,1)S(1)} %dynamic-slice.5), channel_id=1, replica_groups=mesh['rep'=8,'shard'=4] {'rep'}, use_global_device_ids=true, to_apply=%region_22.23 | all-reduce | flops 576 | bytes 2304 | tf_op jit(solution)/shard_map/psum | solution.py:443
  751.3 5.9 fusion.8
  757.2 14.2 %fusion.11 = bf16[1,1024,1152]{2,1,0:T(8,128)(2,1)} fusion(f32[1024,1152]{1,0:T(8,128)} %copy-done.3, bf16[1024,3072]{1,0:T(8,128)(2,1)} %get-tuple-element.53, bf16[3072,1152]{1,0:T(8,128)(2,1)} %all-gather.14.cloned.1.call-done), kind=kOutput, calls=%fused_computation.33 | convolution fusion | flops 7250116608 | bytes 20447232 | tf_op jit(solution)/shard_map/dot_general | solution.py:275
  771.3 137.0 %all-reduce.10.cloned.1.call-done = (bf16[288,1152]{1,0:T(8,128)(2,1)}, bf16[288,384]{1,0:T(8,128)(2,1)}, bf16[288,384]{1,0:T(8,128)(2,1)}, bf16[288,1152]{1,0:T...) async-done(((bf16[288,1152]{1,0:T(8,128)(2,1)}, bf16[288,384]{1,0:T(8,128)(2,1)}, bf16[288,384]{1,0:T(8,128)(2,1)}, ...) | async-done | bytes 7077904 | tf_op jit(solution)/shard_map/psum | solution.py:443
  908.4 3.8 convert_element_type.122
  912.2 2.2 convert_element_type.124
  914.4 2.0 convert_element_type.126
  916.5 1.1 convert_element_type.114
  (136 shorter events, 15.9 us)
Async XLA Ops:
  7.2 4.1 copy-start.24
  7.2 3.5 copy-start.23
  7.2 5.3 copy-start.25
  7.2 5.6 copy-start.26
  7.2 45.6 %all-gather.6.cloned.1.call-start = ((), (), s32[]{:S(2)}) async-start(), calls=%async_computation.7 | async-start | bytes 3317760 | tf_op jit(solution)/shard_map/all_gather | solution.py:311
  8.0 81.6 %all-gather.8.cloned.1.call-start = ((), (), s32[]{:S(2)}) async-start(), calls=%async_computation.8 | async-start | bytes 3317760 | tf_op jit(solution)/shard_map/all_gather | solution.py:314
  8.7 113.7 %all-gather.10.cloned.1.call-start = ((), (), s32[]{:S(2)}) async-start(), calls=%async_computation.9 | async-start | bytes 8847360 | tf_op jit(solution)/shard_map/all_gather | solution.py:335
  9.4 19.0 %copy-start.11 = (bf16[288,384]{1,0:T(8,128)(2,1)S(1)}, bf16[288,384]{1,0:T(8,128)(2,1)}, u32[]{:S(2)}) copy-start(bf16[288,384]{1,0:T(8,128)(2,1)} %param.15) | copy-start | bytes 663556
  9.5 165.3 %all-gather.12.cloned.1.call-start = ((), (), s32[]{:S(2)}) async-start(), calls=%async_computation.10 | async-start | bytes 8847360 | tf_op jit(solution)/shard_map/all_gather | solution.py:336
  10.0 32.6 %copy-start.20 = (bf16[288,384]{1,0:T(8,128)(2,1)S(1)}, bf16[288,384]{1,0:T(8,128)(2,1)}, u32[]{:S(2)}) copy-start(bf16[288,384]{1,0:T(8,128)(2,1)} %param.16) | copy-start | bytes 663556
  10.0 217.0 %all-gather.14.cloned.1.call-start = ((), (), s32[]{:S(2)}) async-start(), calls=%async_computation.11 | async-start | bytes 8847360 | tf_op jit(solution)/shard_map/all_gather | solution.py:337
  10.6 382.3 %reduce-scatter.10.cloned.1.call-start = ((), (), s32[]{:S(2)}) async-start(), calls=%async_computation.13 | async-start | bytes 1105920 | tf_op jit(solution)/shard_map/reduce_scatter | solution.py:429
  21.5 0.9 copy-start.21
  52.9 36.7 %copy-start = (bf16[1,1024,1152]{2,1,0:T(8,128)(2,1)S(1)}, bf16[1,1024,1152]{2,1,0:T(8,128)(2,1)}, u32[]{:S(2)}) copy-start(bf16[1,1024,1152]{2,1,0:T(8,128)(2,1)} %param.12) | copy-start | bytes 7077892
  95.7 2.1 copy-start.3
  98.4 24.1 %copy-start.8 = (bf16[1024,1152]{1,0:T(8,128)(2,1)}, bf16[1024,1152]{1,0:T(8,128)(2,1)S(1)}, u32[]{:S(2)}) copy-start(bf16[1024,1152]{1,0:T(8,128)(2,1)S(1)} %multiply_convert_fusion.3) | copy-start | bytes 7077892
  136.1 91.0 %copy-start.7 = (bf16[1,1024,1152]{2,1,0:T(8,128)(2,1)S(1)}, bf16[1,1024,1152]{2,1,0:T(8,128)(2,1)}, u32[]{:S(2)}) copy-start(bf16[1,1024,1152]{2,1,0:T(8,128)(2,1)} %param.23) | copy-start | bytes 7077892
  249.0 29.3 %slice-start = ((s8[4718592]{0:T(1024)(128)(4,1)}), s8[4194304]{0:T(1024)(128)(4,1)S(1)}, s32[]{:S(2)}) async-start(s8[4718592]{0:T(1024)(128)(4,1)} %bitcast.65), calls=%async_computation.20 | async-start | bytes 8388608
  263.0 15.3 %slice-start.1 = ((s8[4718592]{0:T(1024)(128)(4,1)}), s8[524288]{0:T(1024)(128)(4,1)S(1)}, s32[]{:S(2)}) async-start(s8[4718592]{0:T(1024)(128)(4,1)} %bitcast.65), calls=%async_computation.21 | async-start | bytes 1048576
  278.3 3.8 copy-start.28
  279.9 2.2 copy-start.2
  331.4 4.7 copy-start.13
  335.6 57.3 %reduce-scatter.12.cloned.1.call-start = ((), (), s32[]{:S(2)}) async-start(), calls=%async_computation.14 | async-start | bytes 1105920 | tf_op jit(solution)/shard_map/reduce_scatter | solution.py:432
  340.1 85.7 %reduce-scatter.8.cloned.1.call-start = ((), (), s32[]{:S(2)}) async-start(), calls=%async_computation.12 | async-start | bytes 3317760 | tf_op jit(solution)/shard_map/reduce_scatter | solution.py:426
  347.5 116.6 %reduce-scatter.14.cloned.1.call-start = ((), (), s32[]{:S(2)}) async-start(), calls=%async_computation.15 | async-start | bytes 3317760 | tf_op jit(solution)/shard_map/reduce_scatter | solution.py:435
  355.4 174.8 %reduce-scatter.16.cloned.1.call-start = ((), (), s32[]{:S(2)}) async-start(), calls=%async_computation.16 | async-start | bytes 8847360 | tf_op jit(solution)/shard_map/reduce_scatter | solution.py:379
  367.8 228.7 %reduce-scatter.18.cloned.1.call-start = ((), (), s32[]{:S(2)}) async-start(), calls=%async_computation.17 | async-start | bytes 8847360 | tf_op jit(solution)/shard_map/reduce_scatter | solution.py:382
  380.5 282.1 %reduce-scatter.20.cloned.1.call-start = ((), (), s32[]{:S(2)}) async-start(), calls=%async_computation.18 | async-start | bytes 8847360 | tf_op jit(solution)/shard_map/reduce_scatter | solution.py:385
  392.8 269.8 %copy-start.1 = (bf16[1,1024,1152]{2,1,0:T(8,128)(2,1)S(1)}, bf16[1,1024,1152]{2,1,0:T(8,128)(2,1)}, u32[]{:S(2)}) copy-start(bf16[1,1024,1152]{2,1,0:T(8,128)(2,1)} %param.12) | copy-start | bytes 7077892
  392.8 515.6 %all-reduce.10.cloned.1.call-start = ((), (), s32[]{:S(2)}) async-start(), calls=%async_computation.19 | async-start | bytes 14155776 | tf_op jit(solution)/shard_map/psum | solution.py:443
  662.6 0.7 copy-start.22
  662.6 46.4 %copy-start.12 = (bf16[288,384]{1,0:T(8,128)(2,1)S(1)}, bf16[288,384]{1,0:T(8,128)(2,1)}, u32[]{:S(2)}) copy-start(bf16[288,384]{1,0:T(8,128)(2,1)} %param.15) | copy-start | bytes 663556
  662.6 47.2 %copy-start.6 = (bf16[288,1152]{1,0:T(8,128)(2,1)S(1)}, bf16[288,1152]{1,0:T(8,128)(2,1)}, u32[]{:S(2)}) copy-start(bf16[288,1152]{1,0:T(8,128)(2,1)} %param.14) | copy-start | bytes 1990660
  708.4 8.9 copy-start.27
  710.9 6.4 copy-start.5
  710.9 6.4 copy-start.15
  717.3 1.5 copy-start.4
  717.3 1.5 copy-start.14
  908.4 3.8 copy-start.10
  908.4 6.1 copy-start.9
  912.2 4.2 copy-start.17
  914.4 3.2 copy-start.16
  914.4 4.3 copy-start.19
  914.4 5.1 copy-start.18
Sparse Core Ops, SparseCore 0:
  9.6 33.1 all-gather.5
  44.4 25.5 all-gather.7
  71.6 50.8 all-gather.9
  123.8 50.8 all-gather.11
  176.1 50.8 all-gather.13
  335.8 24.7 reduce-scatter.9
  363.9 23.8 reduce-scatter.11
  390.9 34.8 reduce-scatter.7
  429.1 34.8 reduce-scatter.13
  466.4 63.6 reduce-scatter.15
  532.9 63.6 reduce-scatter.17
  598.9 63.6 reduce-scatter.19
  669.0 239.3 all-reduce.9

commit v2 on v1

--- a/solution.py
+++ b/solution.py
@@ -226,33 +226,557 @@
     )(first, q, k, v, g, start_row, cosine, sine, cosine, sine)
 
 
-def project_kernel(x_ref, gain_ref, wq_ref, wk_ref, wv_ref, cos_ref, sin_ref, n_ref, q_ref, k_ref, v_ref):
-    x = x_ref[...].astype(f32)
-    rstd = lax.rsqrt(jnp.mean(x * x, axis=-1, keepdims=True) + eps_norm)
-    normed = (x * rstd * gain_ref[...].astype(f32)).astype(bf16)
-    n_ref[...] = normed
-    cosine, sine = cos_ref[...], -sin_ref[...]
-    for w_ref, out_ref in ((wq_ref, q_ref), (wk_ref, k_ref)):
-        u = dot(normed, w_ref[...], NN)
-        for t in range(out_ref.shape[1] // 128):
-            lanes = slice(t * 128, t * 128 + 128)
-            out_ref[:, lanes] = unrotate(u[:, lanes], cosine, sine).astype(bf16)
-    v_ref[...] = dot(normed, wv_ref[...], NN).astype(bf16)
-
-
-def project(x, gain, wq, wk, wv, cosine, sine):
+def cost(flops, arrays):
+    return pl.CostEstimate(
+        flops=int(flops // 8), transcendentals=0, bytes_accessed=int(sum(a.size * a.dtype.itemsize for a in arrays) // 8)
+    )
+
+
+def shape(rows, columns, kind=bf16):
+    return jax.ShapeDtypeStruct((rows, columns), kind)
+
+
+ANY = pl.BlockSpec(memory_space=pl.ANY)
+
+
+class Pieces:
+    def __init__(self, rows, columns):
+        self.rows, self.columns, self.parts = rows, columns, []
+
+    def arrays(self):
+        return [a for a, _, _ in self.parts]
+
+    def places(self):
+        return [(m, h) for _, m, h in self.parts]
+
+
+def piece_copies(refs, places, rows, target, sems, me, columns=None):
+    copies = []
+    for n, (ref, (m, h)) in enumerate(zip(refs, places)):
+        at = jnp.bitwise_xor(me[0], m) * rows
+        if h is not None:
+            at = at + jnp.bitwise_xor(jnp.bitwise_and(me[1], 1), h) * (rows // 2)
+        source = ref if columns is None else ref.at[:, columns]
+        place = target.at[pl.ds(pl.multiple_of(at, 16), ref.shape[0]), :]
+        copies.append(pltpu.make_async_copy(source, place, sems.at[n]))
+    return copies
+
+
+def other_ways(axis, bit):
+    size = lax.axis_size(axis)
+    return [(n, n ^ bit) for n in range(size)]
+
+
+def swap(value, axis, bit):
+    return lax.ppermute(value, axis, other_ways(axis, bit))
+
+
+class Spread(Pieces):
+    def __init__(self, weight, *tokens):
+        rows = weight.shape[0]
+        super().__init__(rows, weight.shape[1])
+        source = then(weight, *tokens) if tokens else weight
+        odd = jnp.bitwise_and(lax.axis_index("rep"), 1)
+        half = lax.dynamic_slice_in_dim(source, odd * (rows // 2), rows // 2, 0)
+        self.near = swap(half, "shard", 2)
+        self.parts = [(weight, 0, None), (swap(source, "shard", 1), 1, None)]
+
+    def forward(self, *tokens):
+        near = then(self.near, *tokens) if tokens else self.near
+        self.far = swap(near, "rep", 1)
+        self.parts += [(near, 2, 0), (swap(near, "shard", 1), 3, 0)]
+
+    def finish(self, *tokens):
+        far = then(self.far, *tokens) if tokens else self.far
+        self.parts += [(far, 2, 1), (swap(far, "shard", 1), 3, 1)]
+
+
+def dense_call(body, me, grid, blocked, resident, weights, outs, name, flops, scratch=()):
+    counts = [len(w.parts) for w in weights]
+
+    def kernel(me_ref, *refs):
+        refs = list(refs)
+
+        def take(n):
+            got = refs[:n]
+            del refs[:n]
+            return got
+
+        b_refs, r_refs = take(len(blocked)), take(len(resident))
+        w_refs = [take(n) for n in counts]
+        o_refs = take(len(outs))
+        targets = take(len(weights))
+        sems = take(len(weights))
+        copies = [
+            piece_copies(r, w.places(), w.rows, t, s, me_ref)
+            for r, w, t, s in zip(w_refs, weights, targets, sems)
+        ]
+
+        @pl.when(pl.program_id(0) == 0)
+        def _():
+            for group in copies:
+                for c in group:
+                    c.start()
+            for group in copies:
+                for c in group:
+                    c.wait()
+
+        body(b_refs, r_refs, targets, o_refs, refs)
+
+    fixed = lambda a: pl.BlockSpec(a.shape, lambda i, s: (0,) * a.ndim, pipeline_mode=pl.Buffered(1))
+    arrays = [a for a, _ in blocked] + list(resident) + [a for w in weights for a in w.arrays()]
+    return pl.pallas_call(
+        kernel,
+        grid_spec=pltpu.PrefetchScalarGridSpec(
+            num_scalar_prefetch=1,
+            grid=(grid,),
+            in_specs=[s for _, s in blocked] + [fixed(a) for a in resident] + [ANY] * sum(counts),
+            out_specs=[s for _, s in outs],
+            scratch_shapes=[pltpu.VMEM((4 * w.rows, w.columns), bf16) for w in weights]
+            + [pltpu.SemaphoreType.DMA((n,)) for n in counts]
+            + list(scratch),
+        ),
+        out_shape=[a for a, _ in outs],
+        cost_estimate=cost(flops, arrays + [a for a, _ in outs]),
+        name=name,
+    )(me, *arrays)
+
+
+ROWS = 256
+
+
+def rows_of(n):
+    return pl.BlockSpec((ROWS, n), lambda i, s: (i, 0))
+
+
+def project(me, x, gain, wq, wkv, cosine, sine):
     length, width = x.shape
-    rows = 256
-    row_block = lambda n: pl.BlockSpec((rows, n), lambda i: (i, 0))
-    fixed = lambda a: pl.BlockSpec(a.shape, lambda i: (0, 0), pipeline_mode=pl.Buffered(1))
+    kv = wkv.columns // 2
+
+    def body(blocked, resident, weights, outs, _):
+        x_ref, cos_ref, sin_ref = blocked
+        n_ref, q_ref, k_ref, v_ref = outs
+        u = x_ref[...].astype(f32)
+        rstd = lax.rsqrt(jnp.mean(u * u, axis=-1, keepdims=True) + eps_norm)
+        normed = (u * rstd * resident[0][...]).astype(bf16)
+        n_ref[...] = normed
+        c, s = cos_ref[...], -sin_ref[...]
+        q = dot(normed, weights[0][...], NN)
+        k = dot(normed, weights[1][...], NN)
+        for out_ref, y in ((q_ref, q), (k_ref, k)):
+            for t in range(out_ref.shape[1] // 128):
+                lanes = slice(t * 128, t * 128 + 128)
+                out_ref[:, lanes] = unrotate(y[:, lanes], c, s).astype(bf16)
+        v_ref[...] = k[:, kv:].astype(bf16)
+
+    outs = [(shape(length, n), rows_of(n)) for n in (width, wq.columns, kv, kv)]
+    blocked = [(x, rows_of(width)), (cosine, rows_of(128)), (sine, rows_of(128))]
+    return dense_call(
+        body, me, length // ROWS, blocked, [gain], [wq, wkv], outs, "project",
+        2 * length * width * (wq.columns + wkv.columns),
+    )
+
+
+def attend_out(me, mixed, x, gain, wo):
+    length, width = x.shape
+
+    def body(blocked, resident, weights, outs, _):
+        r = blocked[1][...].astype(f32) + dot(blocked[0][...], weights[0][...], NN)
+        rstd = lax.rsqrt(jnp.mean(r * r, axis=-1, keepdims=True) + eps_norm)
+        outs[0][...] = r
+        outs[1][...] = (r * rstd * resident[0][...]).astype(bf16)
+
+    outs = [(shape(length, width, f32), rows_of(width)), (shape(length, width), rows_of(width))]
+    blocked = [(mixed, rows_of(mixed.shape[1])), (x, rows_of(width))]
+    return dense_call(
+        body, me, length // ROWS, blocked, [gain], [wo], outs, "attend_out", 2 * length * width * mixed.shape[1]
+    )
+
+
+def feed_forward(me, normed, grad_y, gate, up, down):
+    length, width = normed.shape
+    tile = down.rows
+    steps = gate.columns // tile
+    counts = [len(gate.parts), len(up.parts), len(down.parts)]
+
+    def kernel(me_ref, n_ref, y_ref, *refs):
+        refs = list(refs)
+        g_parts, u_parts, d_parts = (
+            [refs.pop(0) for _ in range(counts[0])],
+            [refs.pop(0) for _ in range(counts[1])],
+            [refs.pop(0) for _ in range(counts[2])],
+        )
+        act_ref, gg_ref, gu_ref, wg, wu, wd, g_sem, u_sem, d_sem = refs
+        step = pl.program_id(0)
+
+        def transfer(t, what):
+            slot = lax.rem(t, 2)
+            columns = pl.ds(pl.multiple_of(t * tile, 128), tile)
+            for parts, w, sem, target in ((g_parts, gate, g_sem, wg), (u_parts, up, u_sem, wu)):
+                for c in piece_copies(parts, w.places(), w.rows, target.at[slot], sem.at[slot], me_ref, columns):
+                    getattr(c, what)()
+            block = jnp.bitwise_xor(me_ref[0], t)
+            odd = jnp.bitwise_and(me_ref[1], 1)
+            for n, (ref, (m, h)) in enumerate(zip(d_parts, down.places())):
+
+                @pl.when(block == m)
+                def _(n=n, ref=ref, h=h):
+                    at = 0 if h is None else pl.multiple_of(jnp.bitwise_xor(odd, h) * (tile // 2), 16)
+                    place = wd.at[slot, pl.ds(at, ref.shape[0]), :]
+                    getattr(pltpu.make_async_copy(ref, place, d_sem.at[slot, n]), what)()
+
+        @pl.when(step == 0)
+        def _():
+            transfer(step, "start")
+
+        @pl.when(step + 1 < steps)
+        def _():
+            transfer(step + 1, "start")
+
+        transfer(step, "wait")
+        slot = lax.rem(step, 2)
+
+        @pl.loop(0, length // ROWS)
+        def _(r):
+            rows = pl.ds(pl.multiple_of(r * ROWS, ROWS), ROWS)
+            n = n_ref[rows, :]
+            g = dot(n, wg[slot], NN)
+            u = dot(n, wu[slot], NN)
+            ga = dot(y_ref[rows, :], wd[slot], NT)
+            s = 1.0 / (1.0 + jnp.exp(-g))
+            swish = g * s
+            act_ref[rows, :] = (swish * u).astype(bf16)
+            gg_ref[rows, :] = (ga * u * s * (1.0 + g * (1.0 - s))).astype(bf16)
+            gu_ref[rows, :] = (ga * swish).astype(bf16)
+
+    whole = pl.BlockSpec((length, width), lambda t, s: (0, 0), pipeline_mode=pl.Buffered(1))
+    out = pl.BlockSpec((length, tile), lambda t, s: (0, t))
+    arrays = gate.arrays() + up.arrays() + down.arrays()
+    outs = [shape(length, gate.columns)] * 3
     return pl.pallas_call(
-        project_kernel,
-        grid=(length // rows,),
-        in_specs=[row_block(width), fixed(gain), fixed(wq), fixed(wk), fixed(wv), row_block(128), row_block(128)],
-        out_specs=[row_block(width), row_block(wq.shape[1]), row_block(wk.shape[1]), row_block(wv.shape[1])],
-        out_shape=[jax.ShapeDtypeStruct((length, n), bf16) for n in (width, wq.shape[1], wk.shape[1], wv.shape[1])],
-        name="project",
-    )(x, gain, wq, wk, wv, cosine, sine)
+        kernel,
+        grid_spec=pltpu.PrefetchScalarGridSpec(
+            num_scalar_prefetch=1,
+            grid=(steps,),
+            in_specs=[whole, whole] + [ANY] * len(arrays),
+            out_specs=[out] * 3,
+            scratch_shapes=[
+                pltpu.VMEM((2, width, tile), bf16),
+                pltpu.VMEM((2, width, tile), bf16),
+                pltpu.VMEM((2, tile, width), bf16),
+            ]
+            + [pltpu.SemaphoreType.DMA((2, n)) for n in counts],
+        ),
+        out_shape=outs,
+        cost_estimate=cost(6 * length * width * gate.columns, [normed, grad_y] + arrays + outs),
+        name="feed_forward",
+    )(me, normed, grad_y, *arrays)
+
+
+def norm_backward(grad, unit, rstd, gain):
+    scaled = grad * gain
+    return rstd * (scaled - unit * jnp.mean(scaled * unit, axis=-1, keepdims=True))
+
+
+def add_rows(ref, value):
+    @pl.when(pl.program_id(0) == 0)
+    def _():
+        ref[...] = jnp.zeros_like(ref)
+
+    ref[...] += jnp.sum(value, axis=0, keepdims=True)
+
+
+def feed_forward_back(me, grad_gate, grad_up, residual, grad_y, gain, gate, up, wo):
+    length, width = residual.shape
+
+    def body(blocked, resident, weights, outs, _):
+        gs = dot(blocked[0][...], weights[0][...], NT) + dot(blocked[1][...], weights[1][...], NT)
+        r = blocked[2][...]
+        rstd = lax.rsqrt(jnp.mean(r * r, axis=-1, keepdims=True) + eps_norm)
+        unit = r * rstd
+        add_rows(outs[3], gs * unit)
+        gr = norm_backward(gs, unit, rstd, resident[0][...]) + blocked[3][...].astype(f32)
+        low = gr.astype(bf16)
+        outs[0][...] = gr
+        outs[1][...] = low
+        outs[2][...] = dot(low, weights[2][...], NT).astype(bf16)
+
+    heads = 4 * wo.rows
+    outs = [
+        (shape(length, width, f32), rows_of(width)),
+        (shape(length, width), rows_of(width)),
+        (shape(length, heads), rows_of(heads)),
+        (shape(1, width, f32), pl.BlockSpec((1, width), lambda i, s: (0, 0))),
+    ]
+    ff = gate.columns
+    blocked = [(grad_gate, rows_of(ff)), (grad_up, rows_of(ff)), (residual, rows_of(width)), (grad_y, rows_of(width))]
+    return dense_call(
+        body, me, length // ROWS, blocked, [gain], [gate, up, wo], outs, "feed_forward_back",
+        2 * length * width * (2 * ff + heads),
+    )
+
+
+def layer_out(me, activated, residual, down):
+    length, width = residual.shape
+
+    def body(blocked, resident, weights, outs, _):
+        outs[0][...] = (blocked[1][...] + dot(blocked[0][...], weights[0][...], NN)).astype(bf16)
+
+    ff = activated.shape[1]
+    blocked = [(activated, rows_of(ff)), (residual, rows_of(width))]
+    return dense_call(
+        body, me, length // ROWS, blocked, [], [down], [(shape(length, width), rows_of(width))], "layer_out",
+        2 * length * width * ff,
+    )[0]
+
+
+def input_back(me, dq, dk, dv, x, grad_residual, gain, wq, wkv):
+    length, width = x.shape
+
+    def body(blocked, resident, weights, outs, _):
+        kv = jnp.concatenate([blocked[1][...], blocked[2][...]], axis=1)
+        gf = dot(blocked[0][...], weights[0][...], NT) + dot(kv, weights[1][...], NT)
+        u = blocked[3][...].astype(f32)
+        rstd = lax.rsqrt(jnp.mean(u * u, axis=-1, keepdims=True) + eps_norm)
+        unit = u * rstd
+        add_rows(outs[1], gf * unit)
+        outs[0][...] = norm_backward(gf, unit, rstd, resident[0][...]) + blocked[4][...]
+
+    blocked = [(a, rows_of(a.shape[1])) for a in (dq, dk, dv, x, grad_residual)]
+    outs = [
+        (shape(length, width, f32), rows_of(width)),
+        (shape(1, width, f32), pl.BlockSpec((1, width), lambda i, s: (0, 0))),
+    ]
+    return dense_call(
+        body, me, length // ROWS, blocked, [gain], [wq, wkv], outs, "input_back",
+        2 * length * width * (wq.columns + wkv.columns),
+    )
+
+
+def weight_grad(me, left, rights, tile, name):
+    length, rows = left.shape
+    quarter = rows // 4
+    tiles = [r.shape[1] // tile for r in rights]
+    firsts = [sum(tiles[:n]) for n in range(len(tiles))]
+    steps = sum(tiles)
+
+    def kernel(me_ref, l_ref, *refs):
+        r_refs, (near_ref, own_ref, cross_ref), held = refs[: len(rights)], refs[len(rights) : -1], refs[-1]
+        step = pl.program_id(0)
+        for first, count, r_ref in zip(firsts, tiles, r_refs):
+
+            @pl.when((step >= first) & (step < first + count))
+            def _(r_ref=r_ref):
+                held[...] = dot(l_ref[...], r_ref[...], TN).astype(bf16)
+
+        def block(m):
+            at = pl.multiple_of(jnp.bitwise_xor(me_ref[0], m) * quarter, 16)
+            return held[pl.ds(at, quarter), :]
+
+        near_ref[:quarter, :] = block(1)
+        near_ref[quarter:, :] = block(3)
+        own_ref[...] = block(0)
+        cross_ref[...] = block(2)
+
+    def right_spec(first, count):
+        return pl.BlockSpec((length, tile), lambda j, s: (0, jnp.clip(j - first, 0, count - 1)))
+
+    heights = (2 * quarter, quarter, quarter)
+    outs = [shape(h, steps * tile) for h in heights]
+    return pl.pallas_call(
+        kernel,
+        grid_spec=pltpu.PrefetchScalarGridSpec(
+            num_scalar_prefetch=1,
+            grid=(steps,),
+            in_specs=[pl.BlockSpec((length, rows), lambda j, s: (0, 0), pipeline_mode=pl.Buffered(1))]
+            + [right_spec(f, c) for f, c in zip(firsts, tiles)],
+            out_specs=[pl.BlockSpec((h, tile), lambda j, s: (0, j)) for h in heights],
+            scratch_shapes=[pltpu.VMEM((rows, tile), bf16)],
+        ),
+        out_shape=outs,
+        cost_estimate=cost(2 * length * rows * steps * tile, [left, *rights] + outs),
+        name=name,
+    )(me, left, *rights)
+
+
+def wide_sum(*values):
+    total = values[0].astype(f32)
+    for v in values[1:]:
+        total = total + v.astype(f32)
+    return total.astype(bf16)
+
+
+def then(values, *tokens):
+    return lax.optimization_barrier((values, tokens))[0]
+
+
+MESH = pl.DeviceIdType.MESH
+
+
+def rep_sums(chunks, small):
+    units, outs, flat, maps = [], [], [], []
+    for terms, unit, order in chunks:
+        where = []
+        for arrays in terms:
+            rows, columns = arrays[0].shape
+            for r in range(rows // unit[0]):
+                for c in range(columns // unit[1]):
+                    where.append((len(flat), len(arrays), r * unit[0], c * unit[1]))
+            flat += arrays
+        maps.append(where)
+        tall = terms[0][0].shape[1] == unit[1]
+        outs.append(shape(unit[0] * 8, unit[1]) if tall else shape(unit[0], unit[1] * 8))
+        units.append((unit, tall, order))
+    count = len(chunks)
+
+    def kernel(*refs):
+        ins, small_ref = refs[: len(flat)], refs[len(flat)]
+        out_refs = refs[len(flat) + 1 : len(flat) + 1 + count]
+        small_out = refs[len(flat) + 1 + count]
+        rest = list(refs[len(flat) + 2 + count :])
+        held = [rest.pop(0) for _ in range(count)]
+        landed = [rest.pop(0) for _ in range(count)]
+        load_sem, send_sem, recv_sem, own_sem, small_held, small_landed, small_send, small_recv = rest
+        me, shard = lax.axis_index("rep"), lax.axis_index("shard")
+        x = lambda d: jnp.bitwise_xor(me, d)
+
+        for c in range(count):
+            for u, (first, terms, r, k) in enumerate(maps[c]):
+                for t in range(terms):
+                    unit = units[c][0]
+                    source = ins[first + t].at[pl.ds(r, unit[0]), pl.ds(k, unit[1])]
+                    pltpu.make_async_copy(source, held[c].at[t, u], load_sem.at[c, t, u]).start()
+        small_held[0] = small_ref[...]
+
+        barrier = pltpu.get_barrier_semaphore()
+        peers = [{"rep": x(1)}, {"rep": x(2)}, {"rep": x(4)}]
+        peers += [{"shard": jnp.bitwise_xor(shard, 1)}, {"shard": jnp.bitwise_xor(shard, 2)}]
+        for peer in peers:
+            pl.semaphore_signal(barrier, inc=1, device_id=peer, device_id_type=MESH)
+        pl.semaphore_wait(barrier, len(peers))
+
+        def send(source, target, c, n, bit):
+            return pltpu.make_async_remote_copy(
+                src_ref=source, dst_ref=target, send_sem=send_sem.at[c, n], recv_sem=recv_sem.at[c, n],
+                device_id={"rep": x(bit)}, device_id_type=MESH,
+            )
+
+        def place(c, u):
+            unit, tall, _ = units[c]
+            if tall:
+                return out_refs[c].at[pl.ds(pl.multiple_of(u * unit[0], 16), unit[0]), :]
+            return out_refs[c].at[:, pl.ds(pl.multiple_of(u * unit[1], 128), unit[1])]
+
+        def plan(c):
+            bits = units[c][2]
+            kept = list(range(8))
+            stages = []
+            for bit in bits:
+                kept = [d for d in kept if not d & bit]
+                stages.append((bit, kept))
+            return stages
+
+        def reduce_copies(c, j):
+            bit, kept = plan(c)[j]
+            first = [0, 4, 6][j]
+            return [send(held[c].at[0, x(d | bit)], landed[c].at[first + i], c, first + i, bit) for i, d in enumerate(kept)]
+
+        def give_copies(c, j):
+            bit, kept = plan(c)[j]
+            first = 7 + [0, 4, 6][j]
+            return [send(place(c, x(d)), place(c, x(d)), c, first + i, bit) for i, d in enumerate(kept)]
+
+        def small_copy(j):
+            return pltpu.make_async_remote_copy(
+                src_ref=small_held.at[j], dst_ref=small_landed.at[j], send_sem=small_send.at[j], recv_sem=small_recv.at[j],
+                device_id=peers[j], device_id_type=MESH,
+            )
+
+        def small_step(j):
+            small_copy(j).wait()
+            a, b = small_held[j], small_landed[j]
+            row = lax.broadcasted_iota(jnp.int32, a.shape, 0)
+            small_held[j + 1] = jnp.where(row == 2, jnp.maximum(a, b), a + b)
+            if j < 4:
+                small_copy(j + 1).start()
+
+        small_copy(0).start()
+        for c in range(count):
+            for u, (first, terms, r, k) in enumerate(maps[c]):
+                for t in range(terms):
+                    unit = units[c][0]
+                    source = ins[first + t].at[pl.ds(r, unit[0]), pl.ds(k, unit[1])]
+                    pltpu.make_async_copy(source, held[c].at[t, u], load_sem.at[c, t, u]).wait()
+            terms = maps[c][0][1]
+
+            @pl.loop(0, 8)
+            def _(u, c=c, terms=terms):
+                held[c][0, u] = wide_sum(*[held[c][t, u] for t in range(terms)])
+
+            for copy in reduce_copies(c, 0):
+                copy.start()
+        for j in range(3):
+            small_step(j)
+            for c in range(count):
+                bit, kept = plan(c)[j]
+                first = [0, 4, 6][j]
+                for i, (d, copy) in enumerate(zip(kept, reduce_copies(c, j))):
+                    copy.wait()
+                    held[c][0, x(d)] = wide_sum(held[c][0, x(d)], landed[c][first + i])
+                if j < 2:
+                    for copy in reduce_copies(c, j + 1):
+                        copy.start()
+                else:
+                    own = pltpu.make_async_copy(held[c].at[0, me], place(c, me), own_sem.at[c])
+                    own.start()
+                    own.wait()
+                    for copy in give_copies(c, 2):
+                        copy.start()
+        for j in (2, 1, 0):
+            if j:
+                small_step(5 - j)
+            for c in range(count):
+                for copy in give_copies(c, j):
+                    copy.wait()
+                if j:
+                    for copy in give_copies(c, j - 1):
+                        copy.start()
+        small_out[...] = small_held[5]
+
+    scratch = [pltpu.VMEM((len(terms[0]), 8) + unit, bf16) for terms, unit, _ in chunks]
+    scratch += [pltpu.VMEM((7,) + unit, bf16) for _, unit, _ in chunks]
+    most = max(len(terms[0]) for terms, _, _ in chunks)
+    scratch += [
+        pltpu.SemaphoreType.DMA((count, most, 8)),
+        pltpu.SemaphoreType.DMA((count, 14)),
+        pltpu.SemaphoreType.DMA((count, 14)),
+        pltpu.SemaphoreType.DMA((count,)),
+        pltpu.VMEM((6,) + small.shape, f32),
+        pltpu.VMEM((5,) + small.shape, f32),
+        pltpu.SemaphoreType.DMA((5,)),
+        pltpu.SemaphoreType.DMA((5,)),
+    ]
+    vmem = pl.BlockSpec(memory_space=pltpu.VMEM)
+    return pl.pallas_call(
+        kernel,
+        in_specs=[ANY] * len(flat) + [vmem],
+        out_specs=[ANY] * count + [vmem],
+        out_shape=outs + [shape(*small.shape, f32)],
+        scratch_shapes=scratch,
+        compiler_params=pltpu.CompilerParams(collective_id=0, has_side_effects=True),
+        name="rep_sums",
+    )(*flat, small)
+
+
+def small_all(value, is_max):
+    for axis in ("shard", "rep"):
+        bit = 1
+        while bit < lax.axis_size(axis):
+            other = swap(value, axis, bit)
+            value = jnp.where(is_max, jnp.maximum(value, other), value + other)
+            bit *= 2
+    return value
+
 
 def positions_of(segment_row):
     position_index = jnp.arange(segment_row.shape[0], dtype=jnp.int32)
@@ -271,20 +795,12 @@
     return jnp.concatenate([cosine] * 4, axis=1), jnp.concatenate([-sine, sine, -sine, sine], axis=1)
 
 
-def product(left, right):
-    return jnp.dot(left, right, preferred_element_type=jnp.float32)
-
-
-def product_left(left, right):
-    return lax.dot_general(
-        left, right, (((0,), (0,)), ((), ())), preferred_element_type=jnp.float32
-    )
-
-
-def product_right(left, right):
-    return lax.dot_general(
-        left, right, (((1,), (1,)), ((), ())), preferred_element_type=jnp.float32
-    )
+def in_order(parts):
+    index = lax.axis_index("shard")
+    even, odd = jnp.bitwise_and(index, 1) == 0, jnp.bitwise_and(index, 2) == 0
+    a, b, c, d = parts
+    a, b, c, d = jnp.where(even, a, b), jnp.where(even, b, a), jnp.where(even, c, d), jnp.where(even, d, c)
+    return [jnp.where(odd, a, c), jnp.where(odd, b, d), jnp.where(odd, c, a), jnp.where(odd, d, b)]
 
 
 def on_device(
@@ -301,147 +817,111 @@
     feedforward_gain,
     upstream,
 ):
-    seq_count, length, model_width = layer_input.shape
-    token_rows = seq_count * length
-    group_size = HEADS // KV_HEADS
-    query_width = HEADS * HEAD_DIM
-    key_width = KV_HEADS * HEAD_DIM
+    _, length, model_width = layer_input.shape
+    query_width, key_width = query_weight.shape[1], key_weight.shape[1]
+    shard, rep = lax.axis_index("shard"), lax.axis_index("rep")
+    me = jnp.stack([shard, rep]).astype(jnp.int32)
+    x, grad_y = layer_input[0], upstream[0]
+
+    gains = jnp.stack([attention_gain, feedforward_gain])
+    gains = jnp.concatenate(
+        in_order([gains] + [swap(gains, "shard", m) for m in (1, 2, 3)]), axis=1
+    ).astype(f32)
+    wkv = Spread(jnp.concatenate([key_weight, value_weight], axis=1))
+    wq = Spread(query_weight)
+    for w in (wkv, wq):
+        w.forward()
+    for w in (wkv, wq):
+        w.finish()
+    wo = Spread(output_weight, wq.near)
+    gate, up, down = (Spread(w, wq.near) for w in (gate_weight, up_weight, down_weight))
+
     position_index = jnp.arange(length, dtype=jnp.int32)
-    query_full, key_full, value_full, output_full, gain_first = (
-        lax.all_gather(query_weight, "shard", axis=0, tiled=True),
-        lax.all_gather(key_weight, "shard", axis=0, tiled=True),
-        lax.all_gather(value_weight, "shard", axis=0, tiled=True),
-        lax.all_gather(output_weight, "shard", axis=0, tiled=True),
-        lax.all_gather(attention_gain, "shard", axis=0, tiled=True),
-    )
-    inputs = layer_input.reshape(token_rows, model_width).astype(jnp.float32)
     places = positions_of(segments[0])
     cosine, sine = rope_tables(places)
     doc_start = position_index - places
     first_block = doc_start[::TQ] // TQ
     most = min(length // TQ, MOST_DOC // TQ + 1)
-    first_rstd = lax.rsqrt(jnp.mean(inputs * inputs, axis=-1, keepdims=True) + eps_norm)
-    first_unit = inputs * first_rstd
-    gain_first_wide = gain_first.astype(jnp.float32)
-    first_normed, queries, keys_rot, values = project(
-        layer_input[0], gain_first[None, :], query_full, key_full, value_full, cosine, sine
-    )
+
+    first_normed, queries, keys, values = project(me, x, gains[:1], wq, wkv, cosine, sine)
+    for w in (wo, gate):
+        w.forward(values)
     mixed, head_top = attention_forward(
-        queries, keys_rot, values, doc_start[:, None], first_block, most
-    )
-    maxima = lax.pmax(head_top, ("rep", "shard"))
-    residual = inputs + product(mixed, output_full)
-    gate_full, up_full, down_full, gain_second = (
-        lax.all_gather(gate_weight, "shard", axis=0, tiled=True),
-        lax.all_gather(up_weight, "shard", axis=0, tiled=True),
-        lax.all_gather(down_weight, "shard", axis=0, tiled=True),
-        lax.all_gather(feedforward_gain, "shard", axis=0, tiled=True),
-    )
-    second_rstd = lax.rsqrt(jnp.mean(residual * residual, axis=-1, keepdims=True) + eps_norm)
-    second_unit = residual * second_rstd
-    gain_second_wide = gain_second.astype(jnp.float32)
-    second_normed = (second_unit * gain_second_wide).astype(jnp.bfloat16)
-    gate_values = product(second_normed, gate_full)
-    up_values = product(second_normed, up_full)
-    sigmoid_gate = jax.nn.sigmoid(gate_values)
-    swish_gate = gate_values * sigmoid_gate
-    activated = (swish_gate * up_values).astype(jnp.bfloat16)
-    layer_output = (
-        (residual + product(activated, down_full)).astype(jnp.bfloat16).reshape(layer_input.shape)
-    )
-    gate_back, up_back, down_back = (
-        lax.all_gather(gate_weight, "shard", axis=0, tiled=True),
-        lax.all_gather(up_weight, "shard", axis=0, tiled=True),
-        lax.all_gather(down_weight, "shard", axis=0, tiled=True),
-    )
-    grad_output = upstream.reshape(token_rows, model_width).astype(jnp.float32)
-    grad_down_in = grad_output.astype(jnp.bfloat16)
-    grad_activated = product_right(grad_down_in, down_back)
-    grad_gate_low = (
-        grad_activated * up_values * sigmoid_gate * (1.0 + gate_values * (1.0 - sigmoid_gate))
-    ).astype(jnp.bfloat16)
-    grad_up_low = (grad_activated * swish_gate).astype(jnp.bfloat16)
-    down_term = product_left(activated, grad_down_in)
-    gate_term = product_left(second_normed, grad_gate_low)
-    up_term = product_left(second_normed, grad_up_low)
-    grad_second = product_right(grad_gate_low, gate_back) + product_right(grad_up_low, up_back)
-    second_gain_term = jnp.sum(grad_second * second_unit, axis=0)
-    grad_unit_second = grad_second * gain_second_wide
-    grad_residual = (
-        second_rstd
-        * (
-            grad_unit_second
-            - second_unit * jnp.mean(grad_unit_second * second_unit, axis=-1, keepdims=True)
+        then(queries, wo.near, gate.near), keys, values, doc_start[:, None], first_block, most
+    )
+    wo.finish(mixed)
+    gate.finish(mixed)
+    up.forward(mixed)
+    down.forward(mixed)
+    residual, second_normed = attend_out(me, then(mixed, up.near, down.near), x, gains[1:], wo)
+    up.finish(second_normed)
+    down.finish(second_normed)
+    activated, grad_gate, grad_up = feed_forward(me, second_normed, grad_y, gate, up, down)
+
+    class Sum:
+        def __init__(self, blocks):
+            self.near, self.own, self.cross = blocks
+            self.rows = self.own.shape[0]
+            self.got = swap(self.near, "shard", 1)
+
+        def cross_over(self, *tokens):
+            got = then(self.got, *tokens)
+            self.own_near, sent = got, wide_sum(self.cross, got[self.rows :])
+            self.sent = sent
+            self.crossed = swap(sent, "shard", 2)
+
+        def terms(self):
+            return [self.own, self.own_near, self.crossed]
+
+    gate_sum = Sum(weight_grad(me, second_normed, [grad_gate], 512, "gate_grad"))
+    up_sum = Sum(weight_grad(me, then(second_normed, gate_sum.own), [grad_up], 512, "up_grad"))
+    gate_sum.cross_over(up_sum.own)
+    down_sum = Sum(weight_grad(me, then(activated, gate_sum.sent), [grad_y], 384, "down_grad"))
+    up_sum.cross_over(down_sum.own)
+    grad_residual, grad_low, grad_mixed, second_gain = feed_forward_back(
+        me, then(grad_gate, up_sum.sent), grad_up, residual, grad_y, gains[1:], gate, up, wo
+    )
+    down_sum.cross_over(grad_low)
+    output_sum = Sum(weight_grad(me, then(mixed, down_sum.sent), [grad_low], 384, "output_grad"))
+    dq, dk, dv = attention_backward(
+        then(queries, output_sum.own, gate_sum.crossed), keys, values, grad_mixed, doc_start[None, :], cosine, sine, first_block, most
+    )
+    output_sum.cross_over(dq)
+    qkv_sum = Sum(weight_grad(me, then(first_normed, output_sum.sent, up_sum.crossed), [dq, dk, dv], 384, "qkv_grad"))
+    input_grad, first_gain = input_back(
+        me, then(dq, qkv_sum.own), dk, dv, x, grad_residual, gains[:1], wq, wkv
+    )
+    qkv_sum.cross_over(first_gain)
+    layer_output = layer_out(me, then(activated, qkv_sum.sent, down_sum.crossed, output_sum.crossed), residual, down)
+
+    top = jnp.full((1, model_width), -1e30, f32).at[0, :HEADS].set(head_top)
+    small = jnp.concatenate([first_gain, second_gain, top, jnp.zeros((5, model_width), f32)], axis=0)
+    if lax.axis_size("rep") == 8:
+        wide, narrow = (gate_sum.rows, gate_weight.shape[1] // 8), (down_sum.rows // 8, model_width)
+        chunks = [
+            ([gate_sum.terms()], wide, (1, 2, 4)),
+            ([up_sum.terms()], wide, (2, 4, 1)),
+            ([down_sum.terms()], narrow, (1, 2, 4)),
+            ([output_sum.terms(), qkv_sum.terms()], wide, (2, 4, 1)),
+        ]
+        gate_grad, up_grad, down_grad, attention, small = rep_sums(chunks, then(small, layer_output))
+        output_grad, qkv_grad = attention[:, :model_width], attention[:, model_width:]
+    else:
+        gate_grad, up_grad, down_grad, output_grad, qkv_grad = (
+            lax.psum(wide_sum(v.own, v.own_near[: v.rows], v.crossed), "rep") for v in (gate_sum, up_sum, down_sum, output_sum, qkv_sum)
         )
-        + grad_output
-    )
-    feedforward_sums = (
-        lax.psum_scatter(
-            gate_term.astype(jnp.bfloat16), "shard", scatter_dimension=0, tiled=True
-        ),
-        lax.psum_scatter(
-            up_term.astype(jnp.bfloat16), "shard", scatter_dimension=0, tiled=True
-        ),
-        lax.psum_scatter(
-            down_term.astype(jnp.bfloat16), "shard", scatter_dimension=0, tiled=True
-        ),
-        lax.psum_scatter(
-            second_gain_term.astype(jnp.bfloat16), "shard", scatter_dimension=0, tiled=True
-        ),
-    )
-    gate_grad, up_grad, down_grad, feedforward_gain_grad = (
-        lax.psum(part, "rep").astype(jnp.float32) for part in feedforward_sums
-    )
-    query_back, key_back, value_back, output_back = (
-        lax.all_gather(query_weight, "shard", axis=0, tiled=True),
-        lax.all_gather(key_weight, "shard", axis=0, tiled=True),
-        lax.all_gather(value_weight, "shard", axis=0, tiled=True),
-        lax.all_gather(output_weight, "shard", axis=0, tiled=True),
-    )
-    grad_out_in = grad_residual.astype(jnp.bfloat16)
-    output_term = product_left(mixed, grad_out_in)
-    grad_mixed = product_right(grad_out_in, output_back).astype(jnp.bfloat16)
-    query_low, key_low, value_low = attention_backward(
-        queries, keys_rot, values, grad_mixed, doc_start[None, :], cosine, sine, first_block, most
-    )
-    query_term = product_left(first_normed, query_low)
-    key_term = product_left(first_normed, key_low)
-    value_term = product_left(first_normed, value_low)
-    grad_first = (
-        product_right(query_low, query_back)
-        + product_right(key_low, key_back)
-        + product_right(value_low, value_back)
-    )
-    first_gain_term = jnp.sum(grad_first * first_unit, axis=0)
-    grad_unit_first = grad_first * gain_first_wide
-    input_grad = (
-        first_rstd
-        * (
-            grad_unit_first
-            - first_unit * jnp.mean(grad_unit_first * first_unit, axis=-1, keepdims=True)
-        )
-        + grad_residual
-    )
-    attention_sums = (
-        lax.psum_scatter(
-            query_term.astype(jnp.bfloat16), "shard", scatter_dimension=0, tiled=True
-        ),
-        lax.psum_scatter(
-            key_term.astype(jnp.bfloat16), "shard", scatter_dimension=0, tiled=True
-        ),
-        lax.psum_scatter(
-            value_term.astype(jnp.bfloat16), "shard", scatter_dimension=0, tiled=True
-        ),
-        lax.psum_scatter(
-            output_term.astype(jnp.bfloat16), "shard", scatter_dimension=0, tiled=True
-        ),
-        lax.psum_scatter(
-            first_gain_term.astype(jnp.bfloat16), "shard", scatter_dimension=0, tiled=True
-        ),
-    )
-    query_grad, key_grad, value_grad, output_grad, attention_gain_grad = (
-        lax.psum(part, "rep").astype(jnp.float32) for part in attention_sums
-    )
+        small = small_all(small, jnp.arange(8)[:, None] == 2)
+    gate_grad, up_grad, down_grad, output_grad, qkv_grad = (
+        v.astype(f32) for v in (gate_grad, up_grad, down_grad, output_grad, qkv_grad)
+    )
+    maxima = small[2, :HEADS]
+    own = attention_gain.shape[0]
+    attention_gain_grad = lax.dynamic_slice(small[0], (shard * own,), (own,))
+    feedforward_gain_grad = lax.dynamic_slice(small[1], (shard * own,), (own,))
+    query_grad = qkv_grad[:, :query_width]
+    key_grad = qkv_grad[:, query_width : query_width + key_width]
+    value_grad = qkv_grad[:, query_width + key_width : query_width + 2 * key_width]
+    group_size = HEADS // KV_HEADS
     query_factor = jnp.sqrt(clip_tau / jnp.maximum(maxima, clip_tau))
     key_factor = jnp.sqrt(
         clip_tau / jnp.maximum(jnp.max(maxima.reshape(KV_HEADS, group_size), axis=1), clip_tau)
@@ -456,7 +936,7 @@
         * key_factor[None, :, None]
     ).reshape(local_rows, key_width)
     return (
-        layer_output,
+        layer_output.reshape(layer_input.shape),
         input_grad.reshape(layer_input.shape),
         query_grad,
         key_grad,

time: 932 us -> 707 us (0.76)
  Pallas kernels: 81.1 us -> 462 us
  waiting for transfers between devices: 511 us -> 148 us
  matrix products: 176 us -> 0 us
  blocking collectives: 104 us -> 0 us
  starting transfers between devices: 1.1 us -> 22.1 us
  local copies, waits for them, and re-layouts: 7.36 us -> 24.1 us
  between operations: 15.9 us -> 1.46 us
  other arithmetic: 31.3 us -> 41.3 us
    pallas_call x1 -> x12, Pallas kernels: 10.8 us -> 391 us  [the longest x1 198 us: rep_sums(): pl.pallas_call(kernel, in_specs=[ANY] * len(flat) + [vmem], out_specs=[AN...]
    reduce_scatter x7 -> x0, waiting for transfers between devices: 270 us -> none  [the longest x1 66.3 us: on_device(): lax.psum_scatter(up_term.astype(jnp.bfloat16), 'shard', scatter_dimension...]
    dot_general x18 -> x0, matrix products: 176 us -> none  [the longest x7 67.3 us: product_right(): lax.dot_general(left, right, (((1,), (1,)), ((), ())), preferred_element_...]
    ppermute x0 -> x43, waiting for transfers between devices: none -> 148 us  [swap(): return lax.ppermute(value, axis, other_ways(axis, bit))]
    psum x1 -> x0, waiting for transfers between devices: 137 us -> none  [on_device(): lax.psum(part, 'rep').astype(jnp.float32)]
    all_gather x5 -> x0, waiting for transfers between devices: 101 us -> none  [the longest x1 38.7 us: on_device(): lax.all_gather(up_weight, 'shard', axis=0, tiled=True)]
    pmax x1 -> x0, blocking collectives: 43.1 us -> none  [on_device(): maxima = lax.pmax(head_top, ('rep', 'shard'))]
    all_gather x2 -> x0, blocking collectives: 24.4 us -> none  [the longest x1 14.1 us: on_device(): lax.all_gather(key_weight, 'shard', axis=0, tiled=True)]
  transfers between devices with their start and end apart: 13 -> 43, of which waited for: 9 -> 15; matrix products, arithmetic and copies ran while one was open for 15% -> 6% of each run, Pallas kernels for 4% -> 29%
where the time goes in v2:
time: 707 us; the launch traced here: 699 us
  Pallas kernels  462 us (65%)
  waiting for transfers between devices  148 us (21%)
  other arithmetic  41.3 us (6%)
  local copies, waits for them, and re-layouts  24.1 us (3%)
  starting transfers between devices  22.1 us (3%)
    pallas_call x1, Pallas kernels, rep_sums(): pl.pallas_call(kernel, in_specs=[ANY] * len(flat) + [vmem], out_specs=[AN...  198 us
    ppermute x43, waiting for transfers between devices, swap(): return lax.ppermute(value, axis, other_ways(axis, bit))  148 us
    pallas_call x5, Pallas kernels, dense_call(): pl.pallas_call(kernel, grid_spec=pltpu.PrefetchScalarGridSpec(num_scalar_...  91.8 us
    pallas_call x5, Pallas kernels, weight_grad(): pl.pallas_call(kernel, grid_spec=pltpu.PrefetchScalarGridSpec(num_scalar_...  63.1 us
    pallas_call x1, Pallas kernels, attention_backward(): pl.pallas_call(functools.partial(backward_kernel, most=most), grid_spec=p...  45.3 us
    pallas_call x1, Pallas kernels, feed_forward(): pl.pallas_call(kernel, grid_spec=pltpu.PrefetchScalarGridSpec(num_scalar_...  37.4 us
    pallas_call x1, Pallas kernels, attention_forward(): pl.pallas_call(functools.partial(forward_kernel, most=most), grid_spec=pl...  26.4 us
    ppermute x43, starting transfers between devices, swap(): return lax.ppermute(value, axis, other_ways(axis, bit))  22.1 us
  transfers between devices with their start and end apart: 43, of which 15 were waited for; matrix products, arithmetic and copies ran while one was open for 6% of the time, Pallas kernels for 29%

profile of v2, /device:TPU:0, one launch (start us, length us, event | category | flops | bytes accessed | tf_op | source)
XLA Modules:
  0.0 698.9 jit_solution(17962574250537501119)
XLA Ops:
  2.0 3.0 collective-permute-start.1
  5.2 1.7 constant_dynamic-slice_fusion.7
  7.0 1.9 collective-permute-start.4
  8.9 1.6 constant_dynamic-update-slice_fusion.1
  10.6 1.6 constant_dynamic-update-slice_fusion.refs_10_.refs_12_
  12.2 1.6 constant_dynamic-slice_fusion.6
  14.6 1.9 fusion
  16.5 1.8 pad_maximum_fusion
  19.8 7.5 %collective-permute-done.9.refs_12_.refs_14_ = bf16[144,768]{1,0:T(8,128)(2,1)} collective-permute-done((bf16[144,768]{1,0:T(8,128)(2,1)}, bf16[144,768]{1,0:T(8,128)(2,1)}, u32[]{:S(2)}, u32[]{:S(2)}) %collective-permute-start.9) | collective-permute-done | bytes 221216 | tf_op jit(solution)/shard_map/ppermute | solution.py:271
  27.4 1.5 collective-permute-start.11
  29.9 2.1 constant_dynamic-slice_fusion.3
  32.5 1.6 collective-permute-done.11.refs_14_.refs_16_
  35.7 1.7 constant_dynamic-slice_fusion.5
  37.9 4.5 collective-permute-done.6.refs_8_.refs_10_
  43.0 1.5 collective-permute-start.14
  47.4 12.7 %project.1 = (bf16[1024,1152]{1,0:T(8,128)(2,1)}, bf16[1024,1152]{1,0:T(8,128)(2,1)}, bf16[1024,384]{1,0:T(8,128)(2,1)}, bf16[1024,384]{1,0:T(8,128)(2,1)}) custom-call(s32[2]{0:T(128)} %pad_add_fusion.me_ref, bf16[1024,1152]{1,0:T(8,128)(2,1)} %bitcast.24, f32[1024,128]{1,0:T(8,128)} %get-tuple-element.179.refs_1_.cos_ref.cosall_ref, ...), custom_call_target="tpu_custom_call" | custom-call | flops 566231040 | bytes 1765952 | tf_op jit(solution)/shard_map/project/pallas_call | solution.py:328
  62.2 1.9 subtract_subtract_fusion.start_ref
  64.1 22.2 %collective-permute-done.14.refs_2_.refs_7_ = bf16[144,3072]{1,0:T(8,128)(2,1)} collective-permute-done((bf16[144,3072]{1,0:T(8,128)(2,1)}, bf16[144,3072]{1,0:T(8,128)(2,1)}, u32[]{:S(2)}, u32[]{:S(2)}) %collective-permute-start.14) | collective-permute-done | bytes 884768 | tf_op jit(solution)/shard_map/ppermute | solution.py:271
  86.3 26.4 %attention_forward.1 = (bf16[1024,1152]{1,0:T(8,128)(2,1)}, f32[8,3,6,8,128]{4,3,2,1,0:T(8,128)}) custom-call(s32[8]{0:T(128)} %and_select_fusion.first_ref, bf16[1024,1152]{1,0:T(8,128)(2,1)} %get-tuple-element.138.q_ref, bf16[1024,384]{1,0:T(8,128)(2,1)} %get-tuple-element.98.k_ref, bf16[1024,384]{1,0:T(8,128)(2,1)} %get-tuple-element.99.v_ref, ...), custom_call_target="tpu_custom_call" | custom-call | tf_op jit(solution)/shard_map/attention_forward/pallas_call | solution.py:94
  115.8 20.2 %collective-permute-done.23.refs_4_.refs_9_ = bf16[144,3072]{1,0:T(8,128)(2,1)} collective-permute-done((bf16[144,3072]{1,0:T(8,128)(2,1)}, bf16[144,3072]{1,0:T(8,128)(2,1)}, u32[]{:S(2)}, u32[]{:S(2)}) %collective-permute-start.23) | collective-permute-done | bytes 884768 | tf_op jit(solution)/shard_map/ppermute | solution.py:271
  136.6 18.4 %collective-permute-done.31.refs_16_.refs_6_ = bf16[384,1152]{1,0:T(8,128)(2,1)} collective-permute-done((bf16[384,1152]{1,0:T(8,128)(2,1)}, bf16[384,1152]{1,0:T(8,128)(2,1)}, u32[]{:S(2)}, u32[]{:S(2)}) %collective-permute-start.31) | collective-permute-done | bytes 884768 | tf_op jit(solution)/shard_map/ppermute | solution.py:271
  155.0 10.1 %attend_out.1 = (f32[1024,1152]{1,0:T(8,128)}, bf16[1024,1152]{1,0:T(8,128)(2,1)}) custom-call(s32[2]{0:T(128)} %pad_add_fusion.me_ref, bf16[1024,1152]{1,0:T(8,128)(2,1)} %get-tuple-element.134.refs_0_.l_ref, bf16[1024,1152]{1,0:T(8,128)(2,1)} %bitcast.25, f32[1,1152]{1,0:T(1,128)} %get-tuple-element.174.refs_2_.refs_4_, bf16[288,1152]{1,0:T(8,128)(2,1)} %refs_17_.1, ...), custom_call_target="tpu_custom_call" | custom-call | flops 339738624 | bytes 1806912 | tf_op jit(solution)/shard_map/attend_out/pallas_call | solution.py:328
  165.1 8.0 %collective-permute-done.27.refs_10_.refs_15_ = bf16[144,3072]{1,0:T(8,128)(2,1)} collective-permute-done((bf16[144,3072]{1,0:T(8,128)(2,1)}, bf16[144,3072]{1,0:T(8,128)(2,1)}, u32[]{:S(2)}, u32[]{:S(2)}) %collective-permute-start.27) | collective-permute-done | bytes 884768 | tf_op jit(solution)/shard_map/ppermute | solution.py:271
  174.2 2.8 collective-permute-done.26.refs_9_.refs_14_
  181.7 37.4 %feed_forward.1 = (bf16[1024,3072]{1,0:T(8,128)(2,1)}, bf16[1024,3072]{1,0:T(8,128)(2,1)}, bf16[1024,3072]{1,0:T(8,128)(2,1)}) custom-call(s32[2]{0:T(128)} %pad_add_fusion.me_ref, bf16[1024,1152]{1,0:T(8,128)(2,1)} %get-tuple-element.119.n_ref.l_ref, bf16[1024,1152]{1,0:T(8,128)(2,1)} %bitcast.21, bf16[288,3072]{1,0:T(8,128)(2,1)} %refs_5_.1, ...), custom_call_target="tpu_custom_call" | custom-call | flops 2717908992 | bytes 5603328 | tf_op jit(solution)/shard_map/feed_forward/pallas_call | solution.py:456
  219.2 13.1 %gate_grad.1 = (bf16[576,3072]{1,0:T(8,128)(2,1)}, bf16[288,3072]{1,0:T(8,128)(2,1)}, bf16[288,3072]{1,0:T(8,128)(2,1)}) custom-call(s32[2]{0:T(128)} %pad_add_fusion.me_ref, bf16[1024,1152]{1,0:T(8,128)(2,1)} %get-tuple-element.119.n_ref.l_ref, bf16[1024,3072]{1,0:T(8,128)(2,1)} %get-tuple-element.130.refs_0_), custom_call_target="tpu_custom_call" | custom-call | flops 905969664 | bytes 1966080 | tf_op jit(solution)/shard_map/gate_grad/pallas_call | solution.py:586
  232.5 13.3 %up_grad.1 = (bf16[576,3072]{1,0:T(8,128)(2,1)}, bf16[288,3072]{1,0:T(8,128)(2,1)}, bf16[288,3072]{1,0:T(8,128)(2,1)}) custom-call(s32[2]{0:T(128)} %pad_add_fusion.me_ref, bf16[1024,1152]{1,0:T(8,128)(2,1)} %get-tuple-element.119.n_ref.l_ref, bf16[1024,3072]{1,0:T(8,128)(2,1)} %get-tuple-element.120.refs_0_.refs_1_), custom_call_target="tpu_custom_call" | custom-call | flops 905969664 | bytes 1966080 | tf_op jit(solution)/shard_map/up_grad/pallas_call | solution.py:586
  246.2 4.6 add_convert_fusion.2
  250.8 16.3 %down_grad.1 = (bf16[1536,1152]{1,0:T(8,128)(2,1)}, bf16[768,1152]{1,0:T(8,128)(2,1)}, bf16[768,1152]{1,0:T(8,128)(2,1)}) custom-call(s32[2]{0:T(128)} %pad_add_fusion.me_ref, bf16[1024,3072]{1,0:T(8,128)(2,1)} %get-tuple-element.152.l_ref.refs_0_, bf16[1024,1152]{1,0:T(8,128)(2,1)} %bitcast.22), custom_call_target="tpu_custom_call" | custom-call | flops 905969664 | bytes 1966080 | tf_op jit(solution)/shard_map/down_grad/pallas_call | solution.py:586
  267.8 3.9 add_convert_fusion.1
  271.7 39.3 %feed_forward_back.1 = (f32[1024,1152]{1,0:T(8,128)}, bf16[1024,1152]{1,0:T(8,128)(2,1)}, bf16[1024,1152]{1,0:T(8,128)(2,1)}, f32[1,1152]{1,0:T(1,128)}) custom-call(s32[2]{0:T(128)} %pad_add_fusion.me_ref, bf16[1024,3072]{1,0:T(8,128)(2,1)} %get-tuple-element.130.refs_0_, bf16[1024,3072]{1,0:T(8,128)(2,1)} %get-tuple-element.120.refs_0_.refs_1_, ...), custom_call_target="tpu_custom_call" | custom-call | flops 2151677952 | bytes 5739648 | tf_op jit(solution)/shard_map/feed_forward_back/pallas_call | solution.py:328
  311.0 4.4 add_convert_fusion
  315.4 8.3 %output_grad.1 = (bf16[576,1152]{1,0:T(8,128)(2,1)}, bf16[288,1152]{1,0:T(8,128)(2,1)}, bf16[288,1152]{1,0:T(8,128)(2,1)}) custom-call(s32[2]{0:T(128)} %pad_add_fusion.me_ref, bf16[1024,1152]{1,0:T(8,128)(2,1)} %get-tuple-element.134.refs_0_.l_ref, bf16[1024,1152]{1,0:T(8,128)(2,1)} %get-tuple-element.132.refs_0_), custom_call_target="tpu_custom_call" | custom-call | flops 339738624 | bytes 921600 | tf_op jit(solution)/shard_map/output_grad/pallas_call | solution.py:586
  323.8 1.6 collective-permute-start.38
  325.9 45.3 %attention_backward.1 = (bf16[1024,1152]{1,0:T(8,128)(2,1)}, bf16[1024,384]{1,0:T(8,128)(2,1)}, bf16[1024,384]{1,0:T(8,128)(2,1)}) custom-call(s32[8]{0:T(128)} %and_select_fusion.first_ref, bf16[1024,1152]{1,0:T(8,128)(2,1)} %get-tuple-element.138.q_ref, bf16[1024,384]{1,0:T(8,128)(2,1)} %get-tuple-element.98.k_ref, ...), custom_call_target="tpu_custom_call" | custom-call | tf_op jit(solution)/shard_map/attention_backward/pallas_call | solution.py:196
  371.2 2.6 add_convert_fusion.4
  373.8 12.0 %qkv_grad.1 = (bf16[576,1920]{1,0:T(8,128)(2,1)}, bf16[288,1920]{1,0:T(8,128)(2,1)}, bf16[288,1920]{1,0:T(8,128)(2,1)}) custom-call(s32[2]{0:T(128)} %pad_add_fusion.me_ref, bf16[1024,1152]{1,0:T(8,128)(2,1)} %get-tuple-element.142.l_ref, bf16[1024,1152]{1,0:T(8,128)(2,1)} %get-tuple-element.148.refs_0_, bf16[1024,384]{1,0:T(8,128)(2,1)} %get-tuple-element.143.refs_1_, ...), custom_call_target="tpu_custom_call" | custom-call | flops 566231040 | bytes 1339392 | tf_op jit(solution)/shard_map/qkv_grad/pallas_call | solution.py:586
  386.4 14.2 %input_back.1 = (f32[1024,1152]{1,0:T(8,128)}, f32[1,1152]{1,0:T(1,128)}) custom-call(s32[2]{0:T(128)} %pad_add_fusion.me_ref, bf16[1024,1152]{1,0:T(8,128)(2,1)} %get-tuple-element.148.refs_0_, bf16[1024,384]{1,0:T(8,128)(2,1)} %get-tuple-element.143.refs_1_, bf16[1024,384]{1,0:T(8,128)(2,1)} %get-tuple-element.144.refs_2_, bf16[1024,1152]{1,0:T(8,128)(2,1)} %bitcast.26, ...), custom_call_target="tpu_custom_call" | custom-call | flops 566231040 | bytes 2520192 | tf_op jit(solution)/shard_map/input_back/pallas_call | solution.py:328
  402.2 1.7 collective-permute-start.42
  407.6 20.1 %collective-permute-done.40.refs_8_ = bf16[768,1152]{1,0:T(8,128)(2,1)} collective-permute-done((bf16[768,1152]{1,0:T(8,128)(2,1)}, bf16[768,1152]{1,0:T(8,128)(2,1)}, u32[]{:S(2)}, u32[]{:S(2)}) %collective-permute-start.40) | collective-permute-done | bytes 1769504 | tf_op jit(solution)/shard_map/ppermute | solution.py:271
  427.8 37.4 %collective-permute-done.41.refs_11_ = bf16[288,1152]{1,0:T(8,128)(2,1)} collective-permute-done((bf16[288,1152]{1,0:T(8,128)(2,1)}, bf16[288,1152]{1,0:T(8,128)(2,1)}, u32[]{:S(2)}, u32[]{:S(2)}) %collective-permute-start.41) | collective-permute-done | bytes 663584 | tf_op jit(solution)/shard_map/ppermute | solution.py:271
  465.1 15.4 %layer_out.1 = bf16[1024,1152]{1,0:T(8,128)(2,1)} custom-call(s32[2]{0:T(128)} %pad_add_fusion.me_ref, bf16[1024,3072]{1,0:T(8,128)(2,1)} %get-tuple-element.152.l_ref.refs_0_, f32[1024,1152]{1,0:T(8,128)} %get-tuple-element.131.refs_2_.refs_1_, bf16[768,1152]{1,0:T(8,128)(2,1)} %refs_2_.1, bf16[768,1152]{1,0:T(8,128)(2,1)} %collective-permute-done.29.refs_13_.refs_3_, ...), custom_call_target="tpu_custom_call" | custom-call | flops 905969664 | bytes 2555904 | tf_op jit(solution)/shard_map/layer_out/pallas_call | solution.py:328
  481.5 198.2 %rep_sums.1 = (bf16[288,3072]{1,0:T(8,128)(2,1)}, bf16[288,3072]{1,0:T(8,128)(2,1)}, bf16[768,1152]{1,0:T(8,128)(2,1)}, bf16[288,3072]{1,0:T(8,128)(2,1)}, f32[8,1152]{1,0:T(8,128)}) custom-call(bf16[288,3072]{1,0:T(8,128)(2,1)} %get-tuple-element.118.refs_0_, bf16[576,3072]{1,0:T(8,128)(2,1)} %copy-done.2, ...), custom_call_target="tpu_custom_call" | custom-call | tf_op jit(solution)/shard_map/rep_sums/pallas_call | solution.py:760
  682.6 2.2 slice_convert_fusion.1
  689.7 2.2 convert_multiply_fusion
  692.0 2.2 convert_element_type.95
  694.2 2.2 convert_element_type.96
  696.4 2.0 convert_element_type.97
  (170 shorter events, 38.9 us)
Async XLA Ops:
  2.0 17.0 %collective-permute-start.1 = (bf16[2,288]{1,0:T(2,128)(2,1)S(1)}, bf16[2,288]{1,0:T(2,128)(2,1)S(1)}, u32[]{:S(2)}, u32[]{:S(2)}) collective-permute-start(bf16[2,288]{1,0:T(2,128)(2,1)S(1)} %pad_maximum_fusion.2), channel_id=1, source_target_pairs={{0,2},{1,3},{2,0},{3,1},{4,6},{5,7},{6,4},{7,5},{8,10},{9,11},{10,... | collective-permute-start | bytes 3464 | tf_op jit(solution)/shard_map/ppermute | solution.py:271
  5.0 14.6 %collective-permute-start.2 = (bf16[2,288]{1,0:T(2,128)(2,1)S(1)}, bf16[2,288]{1,0:T(2,128)(2,1)S(1)}, u32[]{:S(2)}, u32[]{:S(2)}) collective-permute-start(bf16[2,288]{1,0:T(2,128)(2,1)S(1)} %pad_maximum_fusion.2), channel_id=1, source_target_pairs={{0,3},{1,2},{2,1},{3,0},{4,7},{5,6},{6,5},{7,4},{8,11},{9,10},{10,... | collective-permute-start | bytes 3464 | tf_op jit(solution)/shard_map/ppermute | solution.py:271
  5.0 14.7 %collective-permute-start = (bf16[2,288]{1,0:T(2,128)(2,1)S(1)}, bf16[2,288]{1,0:T(2,128)(2,1)S(1)}, u32[]{:S(2)}, u32[]{:S(2)}) collective-permute-start(bf16[2,288]{1,0:T(2,128)(2,1)S(1)} %pad_maximum_fusion.2), channel_id=1, source_target_pairs={{0,1},{1,0},{2,3},{3,2},{4,5},{5,4},{6,7},{7,6},{8,9},{9,8},{10,11... | collective-permute-start | bytes 3464 | tf_op jit(solution)/shard_map/ppermute | solution.py:271
  7.0 21.9 %collective-permute-start.4 = (bf16[144,1152]{1,0:T(8,128)(2,1)}, bf16[144,1152]{1,0:T(8,128)(2,1)}, u32[]{:S(2)}, u32[]{:S(2)}) collective-permute-start(bf16[144,1152]{1,0:T(8,128)(2,1)} %constant_dynamic-slice_fusion.7), channel_id=1, source_target_pairs={{0,2},{1,3},{2,0},{3,1},{4,6},{5,7},{6,4},{7,5},{8,10},{9,11},{10,... | collective-permute-start | bytes 995336 | tf_op jit(solution)/shard_map/ppermute | solution.py:271
  12.2 25.2 %collective-permute-start.8 = (bf16[288,768]{1,0:T(8,128)(2,1)}, bf16[288,768]{1,0:T(8,128)(2,1)}, u32[]{:S(2)}, u32[]{:S(2)}) collective-permute-start(bf16[288,768]{1,0:T(8,128)(2,1)} %constant_dynamic-update-slice_fusion.refs_10_.refs_12_), channel_id=1, source_target_pairs={{0,1},{1,0},{2,3},{3,2},{4,5},{5,4},{6,7},{7,6},{8,9},{9,8},{10,11... | collective-permute-start | bytes 1327112 | tf_op jit(solution)/shard_map/ppermute | solution.py:271
  14.6 14.3 %copy-start.1 = (bf16[288,3072]{1,0:T(8,128)(2,1)S(1)}, bf16[288,3072]{1,0:T(8,128)(2,1)}, u32[]{:S(2)}) copy-start(bf16[288,3072]{1,0:T(8,128)(2,1)} %refs_5_.1) | copy-start | bytes 5308420
  19.0 25.4 %collective-permute-start.3 = (bf16[288,1152]{1,0:T(8,128)(2,1)}, bf16[288,1152]{1,0:T(8,128)(2,1)}, u32[]{:S(2)}, u32[]{:S(2)}) collective-permute-start(bf16[288,1152]{1,0:T(8,128)(2,1)} %refs_6_.3), channel_id=1, source_target_pairs={{0,1},{1,0},{2,3},{3,2},{4,5},{5,4},{6,7},{7,6},{8,9},{9,8},{10,11... | collective-permute-start | bytes 1990664 | tf_op jit(solution)/shard_map/ppermute | solution.py:271
  19.6 7.7 %collective-permute-start.9 = (bf16[144,768]{1,0:T(8,128)(2,1)}, bf16[144,768]{1,0:T(8,128)(2,1)}, u32[]{:S(2)}, u32[]{:S(2)}) collective-permute-start(bf16[144,768]{1,0:T(8,128)(2,1)} %constant_dynamic-slice_fusion.6), channel_id=1, source_target_pairs={{0,2},{1,3},{2,0},{3,1},{4,6},{5,7},{6,4},{7,5},{8,10},{9,11},{10,... | collective-permute-start | bytes 663560 | tf_op jit(solution)/shard_map/ppermute | solution.py:271
  19.8 14.3 %copy-start = (bf16[768,1152]{1,0:T(8,128)(2,1)S(1)}, bf16[768,1152]{1,0:T(8,128)(2,1)}, u32[]{:S(2)}) copy-start(bf16[768,1152]{1,0:T(8,128)(2,1)} %refs_2_.1) | copy-start | bytes 5308420
  27.4 6.8 collective-permute-start.11
  28.9 6.3 collective-permute-start.10
  32.0 10.4 %collective-permute-start.6 = (bf16[144,1152]{1,0:T(8,128)(2,1)}, bf16[144,1152]{1,0:T(8,128)(2,1)S(1)}, u32[]{:S(2)}, u32[]{:S(2)}) collective-permute-start(bf16[144,1152]{1,0:T(8,128)(2,1)} %collective-permute-done.4.refs_6_.refs_8_), channel_id=1, source_target_pairs={{0,4},{4,0},{8,12},{12,8},{16,20},{20,16},{24,28},{28,24},{1,5},{5... | collective-permute-start | bytes 995336 | tf_op jit(solution)/shard_map/ppermute | solution.py:271
  34.2 8.8 %collective-permute-start.5 = (bf16[144,1152]{1,0:T(8,128)(2,1)}, bf16[144,1152]{1,0:T(8,128)(2,1)S(1)}, u32[]{:S(2)}, u32[]{:S(2)}) collective-permute-start(bf16[144,1152]{1,0:T(8,128)(2,1)} %collective-permute-done.4.refs_6_.refs_8_), channel_id=1, source_target_pairs={{0,1},{1,0},{2,3},{3,2},{4,5},{5,4},{6,7},{7,6},{8,9},{9,8},{10,11... | collective-permute-start | bytes 995336 | tf_op jit(solution)/shard_map/ppermute | solution.py:271
  35.2 9.8 %collective-permute-start.12 = (bf16[144,768]{1,0:T(8,128)(2,1)S(1)}, bf16[144,768]{1,0:T(8,128)(2,1)S(1)}, u32[]{:S(2)}, u32[]{:S(2)}) collective-permute-start(bf16[144,768]{1,0:T(8,128)(2,1)S(1)} %collective-permute-done.11.refs_14_.refs_16_), channel_id=1, source_target_pairs={{0,1},{1,0},{2,3},{3,2},{4,5},{5,4},{6,7},{7,6},{8,9},{9,8},{10,11... | collective-permute-start | bytes 663560 | tf_op jit(solution)/shard_map/ppermute | solution.py:271
  37.4 22.8 %collective-permute-start.13 = (bf16[144,1152]{1,0:T(8,128)(2,1)}, bf16[144,1152]{1,0:T(8,128)(2,1)}, u32[]{:S(2)}, u32[]{:S(2)}) collective-permute-start(bf16[144,1152]{1,0:T(8,128)(2,1)} %constant_dynamic-slice_fusion.5), channel_id=1, source_target_pairs={{0,2},{1,3},{2,0},{3,1},{4,6},{5,7},{6,4},{7,5},{8,10},{9,11},{10,... | collective-permute-start | bytes 995336 | tf_op jit(solution)/shard_map/ppermute | solution.py:271
  42.4 71.6 %collective-permute-start.15 = (bf16[144,3072]{1,0:T(8,128)(2,1)}, bf16[144,3072]{1,0:T(8,128)(2,1)}, u32[]{:S(2)}, u32[]{:S(2)}) collective-permute-start(bf16[144,3072]{1,0:T(8,128)(2,1)} %constant_dynamic-slice_fusion.3), channel_id=1, source_target_pairs={{0,2},{1,3},{2,0},{3,1},{4,6},{5,7},{6,4},{7,5},{8,10},{9,11},{10,... | collective-permute-start | bytes 2654216 | tf_op jit(solution)/shard_map/ppermute | solution.py:271
  43.0 43.3 %collective-permute-start.14 = (bf16[144,3072]{1,0:T(8,128)(2,1)}, bf16[144,3072]{1,0:T(8,128)(2,1)}, u32[]{:S(2)}, u32[]{:S(2)}) collective-permute-start(bf16[144,3072]{1,0:T(8,128)(2,1)} %constant_dynamic-slice_fusion.4), channel_id=1, source_target_pairs={{0,2},{1,3},{2,0},{3,1},{4,6},{5,7},{6,4},{7,5},{8,10},{9,11},{10,... | collective-permute-start | bytes 2654216 | tf_op jit(solution)/shard_map/ppermute | solution.py:271
  44.5 68.8 %collective-permute-start.16 = (bf16[384,1152]{1,0:T(8,128)(2,1)}, bf16[384,1152]{1,0:T(8,128)(2,1)}, u32[]{:S(2)}, u32[]{:S(2)}) collective-permute-start(bf16[384,1152]{1,0:T(8,128)(2,1)} %constant_dynamic-slice_fusion.2), channel_id=1, source_target_pairs={{0,2},{1,3},{2,0},{3,1},{4,6},{5,7},{6,4},{7,5},{8,10},{9,11},{10,... | collective-permute-start | bytes 2654216 | tf_op jit(solution)/shard_map/ppermute | solution.py:271
  45.0 1.7 collective-permute-start.7
  46.7 67.2 %collective-permute-start.17 = (bf16[288,1152]{1,0:T(8,128)(2,1)}, bf16[288,1152]{1,0:T(8,128)(2,1)}, u32[]{:S(2)}, u32[]{:S(2)}) collective-permute-start(bf16[288,1152]{1,0:T(8,128)(2,1)} %refs_17_.1), channel_id=1, source_target_pairs={{0,1},{1,0},{2,3},{3,2},{4,5},{5,4},{6,7},{7,6},{8,9},{9,8},{10,11... | collective-permute-start | bytes 1990664 | tf_op jit(solution)/shard_map/ppermute | solution.py:271
  60.2 52.5 %collective-permute-start.19 = (bf16[144,1152]{1,0:T(8,128)(2,1)}, bf16[144,1152]{1,0:T(8,128)(2,1)}, u32[]{:S(2)}, u32[]{:S(2)}) collective-permute-start(bf16[144,1152]{1,0:T(8,128)(2,1)} %collective-permute-done.13.refs_5_.refs_19_), channel_id=1, source_target_pairs={{0,4},{4,0},{8,12},{12,8},{16,20},{20,16},{24,28},{28,24},{1,5},{5... | collective-permute-start | bytes 995336 | tf_op jit(solution)/shard_map/ppermute | solution.py:271
  86.3 28.1 %collective-permute-start.18 = (bf16[144,1152]{1,0:T(8,128)(2,1)}, bf16[144,1152]{1,0:T(8,128)(2,1)}, u32[]{:S(2)}, u32[]{:S(2)}) collective-permute-start(bf16[144,1152]{1,0:T(8,128)(2,1)} %collective-permute-done.13.refs_5_.refs_19_), channel_id=1, source_target_pairs={{0,1},{1,0},{2,3},{3,2},{4,5},{5,4},{6,7},{7,6},{8,9},{9,8},{10,11... | collective-permute-start | bytes 995336 | tf_op jit(solution)/shard_map/ppermute | solution.py:271
  112.6 2.2 collective-permute-start.20
  113.2 22.8 %collective-permute-start.23 = (bf16[144,3072]{1,0:T(8,128)(2,1)}, bf16[144,3072]{1,0:T(8,128)(2,1)}, u32[]{:S(2)}, u32[]{:S(2)}) collective-permute-start(bf16[144,3072]{1,0:T(8,128)(2,1)} %collective-permute-done.14.refs_2_.refs_7_), channel_id=1, source_target_pairs={{0,4},{4,0},{8,12},{12,8},{16,20},{20,16},{24,28},{28,24},{1,5},{5... | collective-permute-start | bytes 2654216 | tf_op jit(solution)/shard_map/ppermute | solution.py:271
  113.9 59.2 %collective-permute-start.21 = (bf16[288,3072]{1,0:T(8,128)(2,1)S(1)}, bf16[288,3072]{1,0:T(8,128)(2,1)}, u32[]{:S(2)}, u32[]{:S(2)}) collective-permute-start(bf16[288,3072]{1,0:T(8,128)(2,1)S(1)} %copy-done.1), channel_id=1, source_target_pairs={{0,1},{1,0},{2,3},{3,2},{4,5},{5,4},{6,7},{7,6},{8,9},{9,8},{10,11... | collective-permute-start | bytes 5308424 | tf_op jit(solution)/shard_map/ppermute | solution.py:271
  114.0 59.6 %collective-permute-start.25 = (bf16[288,3072]{1,0:T(8,128)(2,1)}, bf16[288,3072]{1,0:T(8,128)(2,1)}, u32[]{:S(2)}, u32[]{:S(2)}) collective-permute-start(bf16[288,3072]{1,0:T(8,128)(2,1)} %refs_11_.1), channel_id=1, source_target_pairs={{0,1},{1,0},{2,3},{3,2},{4,5},{5,4},{6,7},{7,6},{8,9},{9,8},{10,11... | collective-permute-start | bytes 5308424 | tf_op jit(solution)/shard_map/ppermute | solution.py:271
  114.4 59.3 %collective-permute-start.29 = (bf16[768,1152]{1,0:T(8,128)(2,1)S(1)}, bf16[768,1152]{1,0:T(8,128)(2,1)}, u32[]{:S(2)}, u32[]{:S(2)}) collective-permute-start(bf16[768,1152]{1,0:T(8,128)(2,1)S(1)} %copy-done), channel_id=1, source_target_pairs={{0,1},{1,0},{2,3},{3,2},{4,5},{5,4},{6,7},{7,6},{8,9},{9,8},{10,11... | collective-permute-start | bytes 5308424 | tf_op jit(solution)/shard_map/ppermute | solution.py:271
  114.8 40.2 %collective-permute-start.31 = (bf16[384,1152]{1,0:T(8,128)(2,1)}, bf16[384,1152]{1,0:T(8,128)(2,1)}, u32[]{:S(2)}, u32[]{:S(2)}) collective-permute-start(bf16[384,1152]{1,0:T(8,128)(2,1)} %collective-permute-done.16.refs_14_.refs_4_), channel_id=1, source_target_pairs={{0,4},{4,0},{8,12},{12,8},{16,20},{20,16},{24,28},{28,24},{1,5},{5... | collective-permute-start | bytes 2654216 | tf_op jit(solution)/shard_map/ppermute | solution.py:271
  136.0 37.1 %collective-permute-start.27 = (bf16[144,3072]{1,0:T(8,128)(2,1)}, bf16[144,3072]{1,0:T(8,128)(2,1)}, u32[]{:S(2)}, u32[]{:S(2)}) collective-permute-start(bf16[144,3072]{1,0:T(8,128)(2,1)} %collective-permute-done.15.refs_8_.refs_13_), channel_id=1, source_target_pairs={{0,4},{4,0},{8,12},{12,8},{16,20},{20,16},{24,28},{28,24},{1,5},{5... | collective-permute-start | bytes 2654216 | tf_op jit(solution)/shard_map/ppermute | solution.py:271
  155.0 19.1 %collective-permute-start.22 = (bf16[144,3072]{1,0:T(8,128)(2,1)}, bf16[144,3072]{1,0:T(8,128)(2,1)}, u32[]{:S(2)}, u32[]{:S(2)}) collective-permute-start(bf16[144,3072]{1,0:T(8,128)(2,1)} %collective-permute-done.14.refs_2_.refs_7_), channel_id=1, source_target_pairs={{0,1},{1,0},{2,3},{3,2},{4,5},{5,4},{6,7},{7,6},{8,9},{9,8},{10,11... | collective-permute-start | bytes 2654216 | tf_op jit(solution)/shard_map/ppermute | solution.py:271
  173.1 4.0 collective-permute-start.26
  173.1 4.0 collective-permute-start.30
  173.6 4.6 collective-permute-start.24
  173.7 5.8 collective-permute-start.28
  174.1 6.7 collective-permute-start.32
  232.3 13.9 %collective-permute-start.33 = (bf16[576,3072]{1,0:T(8,128)(2,1)}, bf16[576,3072]{1,0:T(8,128)(2,1)S(1)}, u32[]{:S(2)}, u32[]{:S(2)}) collective-permute-start(bf16[576,3072]{1,0:T(8,128)(2,1)} %get-tuple-element.117), channel_id=1, source_target_pairs={{0,1},{1,0},{2,3},{3,2},{4,5},{5,4},{6,7},{7,6},{8,9},{9,8},{10,11... | collective-permute-start | bytes 10616840 | tf_op jit(solution)/shard_map/ppermute | solution.py:271
  245.8 22.0 %collective-permute-start.35 = (bf16[576,3072]{1,0:T(8,128)(2,1)}, bf16[576,3072]{1,0:T(8,128)(2,1)}, u32[]{:S(2)}, u32[]{:S(2)}) collective-permute-start(bf16[576,3072]{1,0:T(8,128)(2,1)} %get-tuple-element.127), channel_id=1, source_target_pairs={{0,1},{1,0},{2,3},{3,2},{4,5},{5,4},{6,7},{7,6},{8,9},{9,8},{10,11... | collective-permute-start | bytes 10616840 | tf_op jit(solution)/shard_map/ppermute | solution.py:271
  267.1 43.8 %collective-permute-start.34 = (bf16[1536,1152]{1,0:T(8,128)(2,1)}, bf16[1536,1152]{1,0:T(8,128)(2,1)S(1)}, u32[]{:S(2)}, u32[]{:S(2)}) collective-permute-start(bf16[1536,1152]{1,0:T(8,128)(2,1)} %get-tuple-element.125), channel_id=1, source_target_pairs={{0,1},{1,0},{2,3},{3,2},{4,5},{5,4},{6,7},{7,6},{8,9},{9,8},{10,11... | collective-permute-start | bytes 10616840 | tf_op jit(solution)/shard_map/ppermute | solution.py:271
  267.3 58.7 %collective-permute-start.37 = (bf16[288,3072]{1,0:T(8,128)(2,1)}, bf16[288,3072]{1,0:T(8,128)(2,1)}, u32[]{:S(2)}, u32[]{:S(2)}) collective-permute-start(bf16[288,3072]{1,0:T(8,128)(2,1)} %add_convert_fusion.2), channel_id=1, source_target_pairs={{0,2},{1,3},{2,0},{3,1},{4,6},{5,7},{6,4},{7,5},{8,10},{9,11},{10,... | collective-permute-start | bytes 5308424 | tf_op jit(solution)/shard_map/ppermute | solution.py:271
  323.7 47.5 %collective-permute-start.36 = (bf16[576,1152]{1,0:T(8,128)(2,1)}, bf16[576,1152]{1,0:T(8,128)(2,1)S(1)}, u32[]{:S(2)}, u32[]{:S(2)}) collective-permute-start(bf16[576,1152]{1,0:T(8,128)(2,1)} %get-tuple-element.136), channel_id=1, source_target_pairs={{0,1},{1,0},{2,3},{3,2},{4,5},{5,4},{6,7},{7,6},{8,9},{9,8},{10,11... | collective-permute-start | bytes 3981320 | tf_op jit(solution)/shard_map/ppermute | solution.py:271
  323.8 50.1 %collective-permute-start.38 = (bf16[288,3072]{1,0:T(8,128)(2,1)}, bf16[288,3072]{1,0:T(8,128)(2,1)S(1)}, u32[]{:S(2)}, u32[]{:S(2)}) collective-permute-start(bf16[288,3072]{1,0:T(8,128)(2,1)} %add_convert_fusion.1), channel_id=1, source_target_pairs={{0,2},{1,3},{2,0},{3,1},{4,6},{5,7},{6,4},{7,5},{8,10},{9,11},{10,... | collective-permute-start | bytes 5308424 | tf_op jit(solution)/shard_map/ppermute | solution.py:271
  371.2 14.6 %copy-start.9 = (bf16[576,1152]{1,0:T(8,128)(2,1)}, bf16[576,1152]{1,0:T(8,128)(2,1)S(1)}, u32[]{:S(2)}) copy-start(bf16[576,1152]{1,0:T(8,128)(2,1)S(1)} %collective-permute-done.36.refs_10_) | copy-start | bytes 3981316
  385.8 14.9 %collective-permute-start.39 = (bf16[576,1920]{1,0:T(8,128)(2,1)}, bf16[576,1920]{1,0:T(8,128)(2,1)S(1)}, u32[]{:S(2)}, u32[]{:S(2)}) collective-permute-start(bf16[576,1920]{1,0:T(8,128)(2,1)} %get-tuple-element.146), channel_id=1, source_target_pairs={{0,1},{1,0},{2,3},{3,2},{4,5},{5,4},{6,7},{7,6},{8,9},{9,8},{10,11... | collective-permute-start | bytes 6635528 | tf_op jit(solution)/shard_map/ppermute | solution.py:271
  386.0 41.7 %collective-permute-start.40 = (bf16[768,1152]{1,0:T(8,128)(2,1)}, bf16[768,1152]{1,0:T(8,128)(2,1)}, u32[]{:S(2)}, u32[]{:S(2)}) collective-permute-start(bf16[768,1152]{1,0:T(8,128)(2,1)} %add_convert_fusion), channel_id=1, source_target_pairs={{0,2},{1,3},{2,0},{3,1},{4,6},{5,7},{6,4},{7,5},{8,10},{9,11},{10,... | collective-permute-start | bytes 5308424 | tf_op jit(solution)/shard_map/ppermute | solution.py:271
  386.4 14.3 %copy-start.19 = (bf16[288,1920]{1,0:T(8,128)(2,1)S(1)}, bf16[288,1920]{1,0:T(8,128)(2,1)}, u32[]{:S(2)}) copy-start(bf16[288,1920]{1,0:T(8,128)(2,1)} %get-tuple-element.145) | copy-start | bytes 3317764
  400.7 79.8 %copy-start.4 = (bf16[576,1920]{1,0:T(8,128)(2,1)}, bf16[576,1920]{1,0:T(8,128)(2,1)S(1)}, u32[]{:S(2)}) copy-start(bf16[576,1920]{1,0:T(8,128)(2,1)S(1)} %collective-permute-done.39.refs_13_) | copy-start | bytes 6635524
  402.2 78.4 %collective-permute-start.42 = (bf16[288,1920]{1,0:T(8,128)(2,1)}, bf16[288,1920]{1,0:T(8,128)(2,1)S(1)}, u32[]{:S(2)}, u32[]{:S(2)}) collective-permute-start(bf16[288,1920]{1,0:T(8,128)(2,1)} %add_convert_fusion.3), channel_id=1, source_target_pairs={{0,2},{1,3},{2,0},{3,1},{4,6},{5,7},{6,4},{7,5},{8,10},{9,11},{10,... | collective-permute-start | bytes 3317768 | tf_op jit(solution)/shard_map/ppermute | solution.py:271
  405.8 59.3 %collective-permute-start.41 = (bf16[288,1152]{1,0:T(8,128)(2,1)}, bf16[288,1152]{1,0:T(8,128)(2,1)}, u32[]{:S(2)}, u32[]{:S(2)}) collective-permute-start(bf16[288,1152]{1,0:T(8,128)(2,1)} %add_convert_fusion.4), channel_id=1, source_target_pairs={{0,2},{1,3},{2,0},{3,1},{4,6},{5,7},{6,4},{7,5},{8,10},{9,11},{10,... | collective-permute-start | bytes 1990664 | tf_op jit(solution)/shard_map/ppermute | solution.py:271
  (22 other events, 107.5 us)
